TPU v7x, 32 devices: a whole 2x2x4 slice. The times are simulated.
32 devices in a mesh: frame: 8 (over y, x, core), chan: 4 (over z).
Axes of the slice: x: 2, y: 2, z: 4, core: 2. Of those that a mesh axis runs over, the one named last changes fastest.
Arguments:
- latent: bfloat16 [8, 512, 2560], P('frame', 'chan'), may hold values from -6 to 6
- spatial_w: bfloat16 [512, 4608], P('chan'), may hold values from -0.09375 to 0.09375
- spatial_b: float32 [512], P('chan'), may hold values from -0.5 to 0.5
- temporal_w: float32 [3, 512], P(None, 'chan'), may hold values from -3 to 3
- temporal_b: float32 [512], P('chan'), may hold values from -1 to 1
Outputs:
- decoded: bfloat16 [8, 512, 2560], P('frame', 'chan')
All inputs are finite; a program needn't handle non-finite values.
Results may differ from a plain program's by a relative error of at most 0.0048.
Values may be sent and summed in bfloat16 or wider, within the bound.
No kernel may reach another device: no remote copies, remote signals or barrier semaphores. Data moves between devices by JAX's collectives and lax.ppermute only.
A program may use at most 64 MiB of HBM per device.

v0:
```python
import jax
import jax.numpy as jnp
from jax import lax
from jax.sharding import PartitionSpec as P

W = 160


def convolve(image, filters, padding):
    return lax.conv_general_dilated(
        image,
        filters,
        (1, 1),
        padding,
        dimension_numbers=("NCHW", "OIHW", "NCHW"),
        preferred_element_type=jnp.float32,
    )


def three_taps(history, values, temporal_w, temporal_b):
    joined = jnp.concatenate([history, values], axis=0).astype(jnp.float32)
    frames = values.shape[0]
    extra = (1,) * (values.ndim - 2)
    taps = temporal_w.reshape((3, 1, temporal_w.shape[1]) + extra)
    bias = temporal_b.reshape((1, temporal_b.shape[0]) + extra)
    total = (
        bias
        + taps[0] * joined[0:frames]
        + taps[1] * joined[1 : frames + 1]
        + taps[2] * joined[2 : frames + 2]
    )
    return total.astype(jnp.bfloat16)


def shards(latent, spatial_w, spatial_b, temporal_w, temporal_b):
    frames, local_chan, pixels = latent.shape
    rows = pixels // W
    full_chan = spatial_w.shape[1] // 9
    shaped_w = spatial_w.reshape(spatial_w.shape[0], 3, 3, full_chan)
    empty = jnp.zeros((frames, spatial_w.shape[0], pixels), jnp.float32)
    piece = lax.all_gather(latent, "chan", axis=1, tiled=True)
    count = piece.shape[1]
    filters = shaped_w.transpose(0, 3, 1, 2)
    image = piece.reshape(frames, count, rows, W)
    summed = empty + convolve(image, filters, ((1, 1), (1, 1))).reshape(
        frames, spatial_w.shape[0], pixels
    )
    spatial = (summed + spatial_b[None, :, None]).astype(jnp.bfloat16)
    band_count = lax.axis_size("frame")
    banded = spatial.reshape(frames, local_chan, band_count, pixels // band_count)
    band = lax.all_to_all(banded, "frame", split_axis=2, concat_axis=0, tiled=True)
    zeros = jnp.zeros((2,) + band.shape[1:], jnp.bfloat16)
    filtered = three_taps(zeros, band, temporal_w, temporal_b)
    result = lax.all_to_all(filtered, "frame", split_axis=0, concat_axis=2, tiled=True)
    decoded = result.reshape(frames, local_chan, pixels)
    return decoded


def solution(mesh):
    placed = (P("frame", "chan", None), P("chan", None), P("chan"), P(None, "chan"), P("chan"))
    return jax.shard_map(
        shards, mesh=mesh, in_specs=placed, out_specs=P("frame", "chan", None), check_vma=False
    )
```

profile of v0, /device:TPU:0, one launch (start us, length us, event | category | flops | bytes accessed | tf_op | source)
XLA Modules:
  0.0 117.0 jit_solution(8465571282082702788)
XLA Ops:
  6.5 0.0 copy-start
  6.5 0.0 all-gather.2.cloned.1.call-start
  6.5 2.3 %copy.15 = bf16[1,128,2560]{1,2,0:T(8,128)(2,1)} copy(bf16[1,128,2560]{2,1,0:T(8,128)(2,1)} %param.5) | data formatting | bytes 1310720 | tf_op args[0]
  8.8 0.0 all-gather.2.cloned.1.call-update
  8.8 0.0 copy-done
  8.8 0.7 copy.19
  9.6 57.0 %all-gather.2.cloned.1.call-done = bf16[1,512,2560]{1,2,0:T(8,128)(2,1)} async-done(((bf16[1,128,2560]{1,2,0:T(8,128)(2,1)}), bf16[1,512,2560]{1,2,0:T(8,128)(2,1)}) %all-gather.2.cloned.1.call-update) | async-done | bytes 2621456 | tf_op jit(solution)/shard_map/all_gather | solution.py:41
  66.5 3.2 %copy.25 = bf16[512,16,1,160]{0,1,3,2:T(8,128)(2,1)S(1)} copy(bf16[512,16,1,160]{0,3,1,2:T(8,128)(2,1)} %bitcast.42) | data formatting | bytes 5242880
  69.7 0.2 pad.1.clone
  70.0 0.0 copy-start.4
  70.0 1.5 %copy.18 = bf16[512,16,1,8,21]{0,3,4,1,2:T(8,128)(2,1)S(1)} copy(bf16[512,16,1,8,21]{0,1,4,3,2:T(8,128)(2,1)S(1)} %bitcast.39) | data formatting | bytes 5505024 | tf_op jit(solution)/shard_map/conv_general_dilated | solution.py:10
  71.5 0.1 slice.29
  71.6 0.0 copy-done.4
  71.6 6.8 %fusion.9 = f32[16,8,21,128]{3,1,2,0:T(8,128)S(1)} fusion(bf16[128,3,3,512]{0,3,2,1:T(8,128)(2,1)S(1)} %bitcast.45, bf16[512,16,1,7,2]{0,3,4,1,2:T(8,128)(2,1)S(1)} %slice.29, bf16[512,16,1,8,21]{0,3,4,1,2:T(8,128)(2,1)S(1)} %copy.18, pred[8,21]{0,1:T(8,128)(4,1)S(1)} %copy-done.4), kind=kOutput, calls=%fused_computation.9 | convolution fusion | flops 3048161280 | bytes 5537960 | tf_op jit(solution)/shard_map/conv_general_dilated | solution.py:10
  78.4 0.3 copy.20
  78.6 0.1 slice_bitcast_fusion
  78.7 0.0 copy-start.2
  78.7 0.4 copy.21
  79.2 0.2 copy-done.2
  79.4 0.0 copy-start.1
  79.4 1.0 fusion.17
  80.3 3.7 %all-to-all-start = ((bf16[1,128,8,320]{1,3,0,2:T(8,128)(2,1)}), bf16[1,128,8,320]{1,3,0,2:T(8,128)(2,1)S(1)}, u32[]{:S(2)}, u32[]{:S(2)}) async-start(bf16[1,128,8,320]{1,3,0,2:T(8,128)(2,1)} %fusion.17), calls=%async_computation | async-start | bytes 1310720 | tf_op jit(solution)/shard_map/all_to_all | solution.py:51
  84.0 0.0 copy-done.1
  84.0 0.0 copy-start.3
  84.0 11.1 %all-to-all-done = bf16[1,128,8,320]{1,3,0,2:T(8,128)(2,1)S(1)} async-done(((bf16[1,128,8,320]{1,3,0,2:T(8,128)(2,1)}), bf16[1,128,8,320]{1,3,0,2:T(8,128)(2,1)S(1)}, u32[]{:S(2)}, u32[]{:S(2)}) %all-to-all-start) | async-done | bytes 655392 | tf_op jit(solution)/shard_map/all_to_all | solution.py:51
  95.1 0.1 pad_convert_fusion
  95.2 0.0 copy-done.3
  95.2 0.3 fusion.18
  95.6 13.5 %all_to_all.33 = bf16[8,128,1,320]{1,3,2,0:T(8,128)(2,1)S(1)} all-to-all(bf16[8,128,1,320]{1,3,2,0:T(8,128)(2,1)S(1)} %fusion.18), channel_id=1, replica_groups=mesh['frame'=8,'chan'=4] {'frame'}, dimensions={0} | all-to-all | bytes 1310720 | tf_op jit(solution)/shard_map/all_to_all | solution.py:54
  109.1 1.1 copy.24
  (1 shorter events, 0.0 us)
Async XLA Ops:
  6.5 2.3 %copy-start = (bf16[128,4608]{1,0:T(8,128)(2,1)S(1)}, bf16[128,4608]{1,0:T(8,128)(2,1)}, u32[]{:S(2)}) copy-start(bf16[128,4608]{1,0:T(8,128)(2,1)} %param.6) | copy-start | bytes 3538948
  6.5 60.0 %all-gather.2.cloned.1.call-start = ((), (), s32[]{:S(2)}) async-start(), calls=%async_computation.2 | async-start | bytes 3276800 | tf_op jit(solution)/shard_map/all_gather | solution.py:41
  70.0 1.6 %copy-start.4 = (pred[8,21]{0,1:T(8,128)(4,1)S(1)}, pred[8,21]{0,1:T(8,128)(4,1)}, u32[]{:S(2)}) copy-start(pred[8,21]{0,1:T(8,128)(4,1)} %constant.9) | copy-start | bytes 508
  78.7 0.7 copy-start.2
  79.4 4.6 %copy-start.1 = (f32[3,128]{1,0:T(4,128)S(1)}, f32[3,128]{1,0:T(4,128)}, u32[]{:S(2)}) copy-start(f32[3,128]{1,0:T(4,128)} %param.8) | copy-start | bytes 4612
  80.3 14.8 %all-to-all-start = ((bf16[1,128,8,320]{1,3,0,2:T(8,128)(2,1)}), bf16[1,128,8,320]{1,3,0,2:T(8,128)(2,1)S(1)}, u32[]{:S(2)}, u32[]{:S(2)}) async-start(bf16[1,128,8,320]{1,3,0,2:T(8,128)(2,1)} %fusion.17), calls=%async_computation | async-start | bytes 1310720 | tf_op jit(solution)/shard_map/all_to_all | solution.py:51
  84.0 11.2 %copy-start.3 = (f32[128]{0:T(128)S(1)}, f32[128]{0:T(128)}, u32[]{:S(2)}) copy-start(f32[128]{0:T(128)} %param.9) | copy-start | bytes 1540
Sparse Core Ops, SparseCore 0:
  8.9 57.5 all-gather.1
where the time goes:
time: 117 us
  waiting for transfers between devices  68.1 us (58%)
  blocking collectives  13.5 us (12%)
  between operations  13.5 us (12%)
  local copies, waits for them, and re-layouts  10.1 us (9%)
  matrix products  6.76 us (6%)
  starting transfers between devices  3.67 us (3%)
  other arithmetic  1.36 us (1%)
    all_gather x1, waiting for transfers between devices, shards(): piece = lax.all_gather(latent, 'chan', axis=1, tiled=True)  57 us
    all_to_all x1, blocking collectives, shards(): lax.all_to_all(filtered, 'frame', split_axis=0, concat_axis=2, tiled=True)  13.5 us
    all_to_all x1, waiting for transfers between devices, shards(): lax.all_to_all(banded, 'frame', split_axis=2, concat_axis=0, tiled=True)  11.1 us
    conv_general_dilated x1, matrix products, convolve(): lax.conv_general_dilated(image, filters, (1, 1), padding, dimension_numbe...  6.76 us
    unnamed x13, local copies, waits for them, and re-layouts  6.42 us
    all_to_all x1, starting transfers between devices, shards(): lax.all_to_all(banded, 'frame', split_axis=2, concat_axis=0, tiled=True)  3.66 us
    conv_general_dilated x5, local copies, waits for them, and re-layouts, convolve(): lax.conv_general_dilated(image, filters, (1, 1), padding, dimension_numbe...  2.37 us
  transfers between devices with their start and end apart: 2, of which 2 were waited for; matrix products, arithmetic and copies ran while one was open for 1% of the time, Pallas kernels for 0%

commit v1 on v0

v1 whole, which is shorter than its diff:
```python
import functools

import jax
import jax.numpy as jnp
from jax import lax
from jax.experimental import pallas as pl
from jax.experimental.pallas import tpu as pltpu
from jax.sharding import PartitionSpec as P


W = 160
CUTS = (8, 12)


VMEM = pl.BlockSpec(memory_space=pltpu.VMEM)
ANY = pl.BlockSpec(memory_space=pl.ANY)


def three_taps(history, values, temporal_w, temporal_b):
    joined = jnp.concatenate([history, values], axis=0).astype(jnp.float32)
    frames = values.shape[0]
    extra = (1,) * (values.ndim - 2)
    taps = temporal_w.reshape((3, 1, temporal_w.shape[1]) + extra)
    bias = temporal_b.reshape((1, temporal_b.shape[0]) + extra)
    total = (
        bias
        + taps[0] * joined[0:frames]
        + taps[1] * joined[1 : frames + 1]
        + taps[2] * joined[2 : frames + 2]
    )
    return total.astype(jnp.bfloat16)


def gathered(latent, spatial_w, spatial_b, temporal_w, temporal_b):
    frames, local_chan, pixels = latent.shape
    rows = pixels // W
    full_chan = spatial_w.shape[1] // 9
    shaped_w = spatial_w.reshape(spatial_w.shape[0], 3, 3, full_chan)
    piece = lax.all_gather(latent, "chan", axis=1, tiled=True)
    image = piece.reshape(frames, full_chan, rows, W)
    summed = lax.conv_general_dilated(
        image,
        shaped_w.transpose(0, 3, 1, 2),
        (1, 1),
        ((1, 1), (1, 1)),
        dimension_numbers=("NCHW", "OIHW", "NCHW"),
        preferred_element_type=jnp.float32,
    )
    summed = summed.reshape(frames, spatial_w.shape[0], pixels)
    spatial = (summed + spatial_b[None, :, None]).astype(jnp.bfloat16)
    band_count = lax.axis_size("frame")
    banded = spatial.reshape(frames, local_chan, band_count, pixels // band_count)
    band = lax.all_to_all(banded, "frame", split_axis=2, concat_axis=0, tiled=True)
    zeros = jnp.zeros((2,) + band.shape[1:], jnp.bfloat16)
    filtered = three_taps(zeros, band, temporal_w, temporal_b)
    result = lax.all_to_all(filtered, "frame", split_axis=0, concat_axis=2, tiled=True)
    return result.reshape(frames, local_chan, pixels)


def place():
    group, frame = lax.axis_index("chan"), lax.axis_index("frame")
    return group, frame, frame & 1, (frame & 1) == (group & 1), (frame >> 1) & 1


def copies(pairs, sems):
    moves = [pltpu.make_async_copy(a, b, sems.at[n]) for n, (a, b) in enumerate(pairs)]
    for move in moves:
        move.start()
    return moves


def split_kernel(latent_ref, w_ref, b_ref, half_ref, *refs, starts, stops):
    own_refs, (frame_ref, sems) = refs[:-2], refs[-2:]
    side = place()[4]
    half, width = half_ref.shape[0], w_ref.shape[1]
    outs = w_ref.shape[0]
    first = pl.multiple_of(side * half, half)
    moves = copies(
        [
            (w_ref.at[pl.ds(first, half), :], half_ref.at[:, 0:width]),
            (latent_ref.at[0], frame_ref),
        ],
        sems,
    )
    bias = b_ref[...]
    high = bias.astype(jnp.bfloat16)
    rest = bias - high.astype(jnp.float32)
    middle = rest.astype(jnp.bfloat16)
    low = (rest - middle.astype(jnp.float32)).astype(jnp.bfloat16)
    row = lax.broadcasted_iota(jnp.int32, (outs, outs), 0)
    pieces = jnp.where(
        row == 0,
        high.astype(jnp.float32),
        jnp.where(
            row == 1,
            middle.astype(jnp.float32),
            jnp.where(row == 2, low.astype(jnp.float32), 0.0),
        ),
    ).T
    half_ref[:, width:] = jnp.where(side == 0, pieces[0:half], pieces[half:]).astype(jnp.bfloat16)
    moves[1].wait()
    for own_ref, a, b in zip(own_refs, starts, stops):
        own_ref[...] = frame_ref[:, a * W : b * W].T
    moves[0].wait()


def order_kernel(w_ref, b_ref, mine_ref, other_ref, out_ref, bias_ref, rows_ref, sems):
    outs, width = w_ref.shape
    chans = out_ref.shape[1] // 4
    half = outs // 2
    group, _, _, straight, side = place()
    one, two, three = group ^ 1, group ^ 2, group ^ 3
    order = [
        jnp.where(straight, two, one),
        jnp.where(straight, one, two),
        jnp.where(straight, three, group),
        jnp.where(straight, group, three),
    ]

    @pl.when(jnp.logical_not(straight))
    def _():
        for move in copies([(w_ref, rows_ref.at[:, 0:width])], sems):
            move.wait()
        bias_ref[...] = b_ref[...]

    @pl.when(straight)
    def _():
        here = pl.multiple_of(side * half, half)
        there = pl.multiple_of((1 - side) * half, half)
        pairs = [
            (mine_ref, rows_ref.at[pl.ds(here, half), :]),
            (other_ref, rows_ref.at[pl.ds(there, half), :]),
        ]
        for move in copies(pairs, sems):
            move.wait()
        pieces = rows_ref[:, width:].astype(jnp.float32).T
        bias_ref[...] = pieces[0:1] + pieces[1:2] + pieces[2:3]

    for slot in range(4):
        for i in range(3):
            for j in range(3):
                start = pl.multiple_of(((i * 3 + j) * 4 + order[slot]) * chans, chans)
                tile = rows_ref[:, pl.ds(start, chans)]
                out_ref[i, slot * chans : (slot + 1) * chans, j * outs : (j + 1) * outs] = tile.T


def conv_kernel(
    first_ref, crossed_ref, second_ref, own_ref, passed_ref, above_ref, w_ref, b_ref,
    out_ref, tail_ref, x_ref, sems, *, top, low
):
    size, outs = out_ref.shape
    pixels, chans = own_ref.shape
    above = W if top else 2 * W
    straight = place()[3]
    body = slice(above, above + pixels)
    moves = copies(
        [
            (first_ref, x_ref.at[body, 0:chans]),
            (crossed_ref, x_ref.at[body, chans : 2 * chans]),
            (second_ref, x_ref.at[body, 2 * chans : 3 * chans]),
        ],
        sems,
    )
    last = x_ref.at[body, 3 * chans :]

    @pl.when(straight)
    def _():
        pltpu.make_async_copy(own_ref, last, sems.at[3]).start()

    @pl.when(jnp.logical_not(straight))
    def _():
        pltpu.make_async_copy(passed_ref, last, sems.at[3]).start()

    x_ref[0:above, :] = jnp.zeros((W, 4 * chans), x_ref.dtype) if top else above_ref[...]
    if low:
        x_ref[above + pixels :, :] = jnp.zeros((W, 4 * chans), x_ref.dtype)
    for move in moves:
        move.wait()
    pltpu.make_async_copy(own_ref, last, sems.at[3]).wait()
    if not low:
        tail_ref[...] = x_ref[above + pixels - 2 * W : above + pixels, :]
    total = jnp.dot(x_ref[0:size, :], w_ref[0], preferred_element_type=jnp.float32)
    for i in range(1, 3):
        total += jnp.dot(
            x_ref[i * W : i * W + size, :], w_ref[i], preferred_element_type=jnp.float32
        )
    column = lax.broadcasted_iota(jnp.int32, (size, outs), 0) % W
    left = jnp.where(column == 0, 0.0, pltpu.roll(total[:, 0:outs], 1, 0))
    right = jnp.where(column == W - 1, 0.0, pltpu.roll(total[:, 2 * outs :], size - 1, 0))
    out_ref[...] = (left + total[:, outs : 2 * outs] + right + b_ref[...]).astype(out_ref.dtype)


def taps_kernel(values_ref, before_ref, previous_ref, taps_ref, bias_ref, *refs):
    out_ref = refs[-1]
    frame = place()[1]
    before = jnp.where(frame >= 2, before_ref[...].astype(jnp.float32), 0.0)
    previous = jnp.where(frame >= 1, previous_ref[...].astype(jnp.float32), 0.0)
    total = (
        bias_ref[...]
        + taps_ref[0:1, :] * before
        + taps_ref[1:2, :] * previous
        + taps_ref[2:3, :] * values_ref[...].astype(jnp.float32)
    )
    out_ref[...] = total.astype(out_ref.dtype).T


def limit(mib):
    return pltpu.CompilerParams(vmem_limit_bytes=mib << 20)


def split_work(latent, spatial_w, spatial_b, temporal_w, temporal_b):
    _, local_chan, pixels = latent.shape
    outs, width = spatial_w.shape
    rows = pixels // W
    frame_count = lax.axis_size("frame")
    core = lax.axis_index("frame") & 1
    both = ("frame", "chan")

    def table(rule):
        moves = []
        for f in range(frame_count):
            for z in range(4):
                to_z, to_c = rule(z, f % 2)
                moves.append((f * 4 + z, (f - f % 2 + to_c) * 4 + to_z))
        return moves

    near = table(lambda z, c: (z ^ 2, c) if z % 2 == c else (z ^ 1, 1 - c))
    far = table(lambda z, c: (z, 1 - c) if z % 2 == c else (z ^ 3, c))
    home = table(lambda z, c: (z - z % 2 + 1 - c, z % 2))
    out = [(b, a) for a, b in home]
    ahead = [(a, (b + 8) % (4 * frame_count)) for a, b in home]
    pair = [(f, f ^ 1) for f in range(frame_count)]
    across = []
    for f in range(frame_count):
        for z in range(4):
            across.append((f * 4 + z, (f ^ 2 if z % 2 == f % 2 else f) * 4 + z))

    def swap(x):
        return lax.ppermute(x, "frame", pair)

    cuts = [c for c in CUTS if c < rows - 1]
    starts = [0] + [c + 1 for c in cuts]
    stops = [c + 1 for c in cuts] + [rows]
    bias_row = spatial_b.reshape(1, outs)
    mine, *owns = pl.pallas_call(
        functools.partial(split_kernel, starts=starts, stops=stops),
        out_shape=[jax.ShapeDtypeStruct((outs // 2, width + 128), jnp.bfloat16)]
        + [
            jax.ShapeDtypeStruct(((b - a) * W, local_chan), jnp.bfloat16)
            for a, b in zip(starts, stops)
        ],
        in_specs=[ANY, ANY, VMEM],
        out_specs=[VMEM] * (1 + len(starts)),
        scratch_shapes=[
            pltpu.VMEM((local_chan, pixels), jnp.bfloat16),
            pltpu.SemaphoreType.DMA((2,)),
        ],
        compiler_params=limit(8),
        name="split",
    )(latent, spatial_w, bias_row)

    mine = lax.ppermute(mine, both, out)
    other = lax.ppermute(mine, both, across)
    filters, bias = pl.pallas_call(
        order_kernel,
        out_shape=(
            jax.ShapeDtypeStruct((3, 4 * local_chan, 3 * outs), jnp.bfloat16),
            jax.ShapeDtypeStruct((1, outs), jnp.float32),
        ),
        in_specs=[ANY, VMEM, ANY, ANY],
        out_specs=(VMEM, VMEM),
        scratch_shapes=[
            pltpu.VMEM((outs, width + 128), jnp.bfloat16),
            pltpu.SemaphoreType.DMA((2,)),
        ],
        compiler_params=limit(8),
        name="order",
    )(spatial_w, bias_row, mine, other)

    arrived = []
    for own in owns:
        first = lax.ppermute(own, both, near)
        second = lax.ppermute(own, both, far)
        arrived.append((own, first, second))

    decoded, tail, column = None, jnp.zeros((2 * W, 4 * local_chan), jnp.bfloat16), 0
    for k, (own, first, second) in enumerate(arrived):
        crossed = swap(first)
        passed = swap(second)
        low = k == len(arrived) - 1
        size = own.shape[0] - W * (k == 0) + W * low
        done, tail = pl.pallas_call(
            functools.partial(conv_kernel, top=k == 0, low=low),
            out_shape=(
                jax.ShapeDtypeStruct((size, outs), jnp.bfloat16),
                jax.ShapeDtypeStruct((2 * W, 4 * local_chan), jnp.bfloat16),
            ),
            in_specs=[ANY] * 5 + [VMEM] * 3,
            out_specs=(VMEM, VMEM),
            scratch_shapes=[
                pltpu.VMEM((size + 2 * W, 4 * local_chan), jnp.bfloat16),
                pltpu.SemaphoreType.DMA((4,)),
            ],
            compiler_params=limit(20),
            name="conv",
        )(first, crossed, second, own, passed, tail, filters, bias)
        spatial = lax.ppermute(done, both, home)
        before = lax.ppermute(done, both, ahead)
        previous = swap(jnp.where(core == 1, before, spatial))
        held = [] if decoded is None else [decoded]
        block = column // size
        decoded = pl.pallas_call(
            taps_kernel,
            out_shape=jax.ShapeDtypeStruct((outs, pixels), jnp.bfloat16),
            grid=(1,),
            in_specs=[VMEM] * 5 + [ANY] * len(held),
            out_specs=pl.BlockSpec((outs, size), lambda n, block=block: (0, block)),
            input_output_aliases={5: 0} if held else {},
            compiler_params=limit(8),
            name="taps",
        )(spatial, before, previous, temporal_w, temporal_b.reshape(1, outs), *held)
        column += size
    return decoded[None]


def shards(latent, *rest):
    if lax.axis_size("chan") == 4 and lax.axis_size("frame") % 4 == 0 and latent.shape[0] == 1:
        return split_work(latent, *rest)
    return gathered(latent, *rest)


def solution(mesh):
    placed = (P("frame", "chan", None), P("chan", None), P("chan"), P(None, "chan"), P("chan"))
    return jax.shard_map(
        shards, mesh=mesh, in_specs=placed, out_specs=P("frame", "chan", None), check_vma=False
    )
```

time: 117 us -> 68.5 us (0.59)
  waiting for transfers between devices: 68.1 us -> 30.5 us
  starting transfers between devices: 3.67 us -> 24.1 us
  blocking collectives: 13.5 us -> 0 us
  between operations: 13.5 us -> 0.18 us
  Pallas kernels: 0 us -> 10.4 us
  local copies, waits for them, and re-layouts: 10.1 us -> 3.05 us
  matrix products: 6.76 us -> 0 us
  other arithmetic: 1.36 us -> 0.07 us
    all_gather x1 -> x0, waiting for transfers between devices: 57 us -> none  [shards(): piece = lax.all_gather(latent, 'chan', axis=1, tiled=True)]
    ppermute x0 -> x23, waiting for transfers between devices: none -> 30.5 us  [the longest x3 9.73 us: split_work(): before = lax.ppermute(done, both, ahead)]
    ppermute x0 -> x23, starting transfers between devices: none -> 24.1 us  [the longest x3 7.85 us: split_work(): first = lax.ppermute(own, both, near)]
    all_to_all x1 -> x0, blocking collectives: 13.5 us -> none  [shards(): lax.all_to_all(filtered, 'frame', split_axis=0, concat_axis=2, tiled=True)]
    all_to_all x1 -> x0, waiting for transfers between devices: 11.1 us -> none  [shards(): lax.all_to_all(banded, 'frame', split_axis=2, concat_axis=0, tiled=True)]
    pallas_call x0 -> x8, Pallas kernels: none -> 10.4 us  [the longest x3 6.15 us: split_work(): pl.pallas_call(functools.partial(conv_kernel, top=k == 0, low=low), out_s...]
    conv_general_dilated x1 -> x0, matrix products: 6.76 us -> none  [convolve(): lax.conv_general_dilated(image, filters, (1, 1), padding, dimension_numbe...]
    all_to_all x1 -> x0, starting transfers between devices: 3.66 us -> none  [shards(): lax.all_to_all(banded, 'frame', split_axis=2, concat_axis=0, tiled=True)]
  transfers between devices with their start and end apart: 2 -> 23, of which waited for: 2 -> 8; matrix products, arithmetic and copies ran while one was open for 1% -> 0% of each run, Pallas kernels for 0% -> 13%
where the time goes in v1:
time: 68.5 us; the launch traced here: 68.2 us
  waiting for transfers between devices  30.5 us (45%)
  starting transfers between devices  24.1 us (35%)
  Pallas kernels  10.4 us (15%)
  local copies, waits for them, and re-layouts  3.05 us (4%)
    ppermute x3, waiting for transfers between devices, split_work(): before = lax.ppermute(done, both, ahead)  9.73 us
    ppermute x3, waiting for transfers between devices, split_work(): first = lax.ppermute(own, both, near)  8.25 us
    ppermute x3, starting transfers between devices, split_work(): first = lax.ppermute(own, both, near)  7.85 us
    ppermute x1, waiting for transfers between devices, split_work(): mine = lax.ppermute(mine, both, out)  7.17 us
    pallas_call x3, Pallas kernels, split_work(): pl.pallas_call(functools.partial(conv_kernel, top=k == 0, low=low), out_s...  6.15 us
    ppermute x3, waiting for transfers between devices, split_work(): second = lax.ppermute(own, both, far)  5.13 us
    ppermute x1, starting transfers between devices, split_work(): other = lax.ppermute(mine, both, across)  3.99 us
    ppermute x3, starting transfers between devices, split_work(): before = lax.ppermute(done, both, ahead)  3.62 us
  transfers between devices with their start and end apart: 23, of which 8 were waited for; matrix products, arithmetic and copies ran while one was open for 0% of the time, Pallas kernels for 13%

profile of v1, /device:TPU:0, one launch (start us, length us, event | category | flops | bytes accessed | tf_op | source)
XLA Modules:
  0.0 68.2 jit_solution(3241016004835240791)
XLA Ops:
  0.0 1.3 %copy-done = bf16[128,4608]{1,0:T(8,128)(2,1)S(1)} copy-done((bf16[128,4608]{1,0:T(8,128)(2,1)S(1)}, bf16[128,4608]{1,0:T(8,128)(2,1)}, u32[]{:S(2)}) %copy-start) | copy-done | bytes 1179672
  1.3 1.1 %copy-done.2 = bf16[1,128,2560]{2,1,0:T(8,128)(2,1)S(1)} copy-done((bf16[1,128,2560]{2,1,0:T(8,128)(2,1)S(1)}, bf16[1,128,2560]{2,1,0:T(8,128)(2,1)}, u32[]{:S(2)}) %copy-start.2) | copy-done | bytes 655384
  2.4 0.7 copy-done.5
  3.0 0.8 %split.1 = (bf16[64,4736]{1,0:T(8,128)(2,1)S(1)}, bf16[1440,128]{1,0:T(8,128)(2,1)S(1)}, bf16[640,128]{1,0:T(8,128)(2,1)S(1)}, bf16[480,128]{1,0:T(8,128)(2,1)S(1)}) custom-call(bf16[1,128,2560]{2,1,0:T(8,128)(2,1)S(1)} %copy-done.2, bf16[128,4608]{1,0:T(8,128)(2,1)S(1)} %copy-done, f32[1,128]{1,0:T(1,128)S(1)} %bitcast.6), custom_call_target="tpu_custom_call" | custom-call | tf_op jit(solution)/shard_map/split/pallas_call | solution.py:245
  3.8 0.6 collective-permute-start.12
  4.4 2.1 %collective-permute-start.10 = (bf16[1440,128]{1,0:T(8,128)(2,1)S(1)}, bf16[1440,128]{1,0:T(8,128)(2,1)S(1)}, u32[]{:S(2)}, u32[]{:S(2)}) collective-permute-start(bf16[1440,128]{1,0:T(8,128)(2,1)S(1)} %get-tuple-element.18.own_ref), channel_id=1, source_target_pairs={{0,4},{1,2},{2,6},{3,0},{4,7},{5,1},{6,5},{7,3},{8,12},{9,10},{10,... | collective-permute-start | bytes 1105928 | tf_op jit(solution)/shard_map/ppermute | solution.py:283
  6.5 2.6 %collective-permute-start.8 = (bf16[1440,128]{1,0:T(8,128)(2,1)S(1)}, bf16[1440,128]{1,0:T(8,128)(2,1)S(1)}, u32[]{:S(2)}, u32[]{:S(2)}) collective-permute-start(bf16[1440,128]{1,0:T(8,128)(2,1)S(1)} %get-tuple-element.18.own_ref), channel_id=1, source_target_pairs={{0,2},{1,4},{2,0},{3,6},{4,1},{5,7},{6,3},{7,5},{8,10},{9,12},{10,... | collective-permute-start | bytes 1105928 | tf_op jit(solution)/shard_map/ppermute | solution.py:282
  9.1 7.2 %collective-permute-done.12.mine_ref = bf16[64,4736]{1,0:T(8,128)(2,1)S(1)} collective-permute-done((bf16[64,4736]{1,0:T(8,128)(2,1)S(1)}, bf16[64,4736]{1,0:T(8,128)(2,1)S(1)}, u32[]{:S(2)}, u32[]{:S(2)}) %collective-permute-start.12) | collective-permute-done | bytes 606240 | tf_op jit(solution)/shard_map/ppermute | solution.py:262
  16.2 4.0 %collective-permute-start.13 = (bf16[64,4736]{1,0:T(8,128)(2,1)S(1)}, bf16[64,4736]{1,0:T(8,128)(2,1)S(1)}, u32[]{:S(2)}, u32[]{:S(2)}) collective-permute-start(bf16[64,4736]{1,0:T(8,128)(2,1)S(1)} %collective-permute-done.12.mine_ref), channel_id=1, source_target_pairs={{0,8},{1,1},{2,10},{3,3},{4,4},{5,13},{6,6},{7,15},{8,0},{9,9},{10... | collective-permute-start | bytes 1818632 | tf_op jit(solution)/shard_map/ppermute | solution.py:263
  20.2 5.1 %collective-permute-done.10.second_ref = bf16[1440,128]{1,0:T(8,128)(2,1)S(1)} collective-permute-done((bf16[1440,128]{1,0:T(8,128)(2,1)S(1)}, bf16[1440,128]{1,0:T(8,128)(2,1)S(1)}, u32[]{:S(2)}, u32[]{:S(2)}) %collective-permute-start.10) | collective-permute-done | bytes 368672 | tf_op jit(solution)/shard_map/ppermute | solution.py:283
  25.4 1.1 %collective-permute-start = (bf16[480,128]{1,0:T(8,128)(2,1)S(1)}, bf16[480,128]{1,0:T(8,128)(2,1)S(1)}, u32[]{:S(2)}, u32[]{:S(2)}) collective-permute-start(bf16[480,128]{1,0:T(8,128)(2,1)S(1)} %get-tuple-element.16.own_ref), channel_id=1, source_target_pairs={{0,2},{1,4},{2,0},{3,6},{4,1},{5,7},{6,3},{7,5},{8,10},{9,12},{10,... | collective-permute-start | bytes 368648 | tf_op jit(solution)/shard_map/ppermute | solution.py:282
  26.9 4.1 %collective-permute-start.4 = (bf16[640,128]{1,0:T(8,128)(2,1)S(1)}, bf16[640,128]{1,0:T(8,128)(2,1)S(1)}, u32[]{:S(2)}, u32[]{:S(2)}) collective-permute-start(bf16[640,128]{1,0:T(8,128)(2,1)S(1)} %get-tuple-element.17.own_ref), channel_id=1, source_target_pairs={{0,2},{1,4},{2,0},{3,6},{4,1},{5,7},{6,3},{7,5},{8,10},{9,12},{10,... | collective-permute-start | bytes 491528 | tf_op jit(solution)/shard_map/ppermute | solution.py:282
  31.1 0.6 collective-permute-done.first_ref
  31.7 7.7 %collective-permute-done.4.first_ref = bf16[640,128]{1,0:T(8,128)(2,1)S(1)} collective-permute-done((bf16[640,128]{1,0:T(8,128)(2,1)S(1)}, bf16[640,128]{1,0:T(8,128)(2,1)S(1)}, u32[]{:S(2)}, u32[]{:S(2)}) %collective-permute-start.4) | collective-permute-done | bytes 163872 | tf_op jit(solution)/shard_map/ppermute | solution.py:282
  39.3 0.5 collective-permute-start.7
  39.9 0.9 %collective-permute-start.1 = (bf16[480,128]{1,0:T(8,128)(2,1)S(1)}, bf16[480,128]{1,0:T(8,128)(2,1)S(1)}, u32[]{:S(2)}, u32[]{:S(2)}) collective-permute-start(bf16[480,128]{1,0:T(8,128)(2,1)S(1)} %collective-permute-done.first_ref), channel_id=1, source_target_pairs={{0,4},{4,0},{8,12},{12,8},{16,20},{20,16},{24,28},{28,24},{1,5},{5... | collective-permute-start | bytes 368648 | tf_op jit(solution)/shard_map/ppermute | solution.py:239
  40.8 0.7 %order.1 = (bf16[3,512,384]{2,1,0:T(8,128)(2,1)S(1)}, f32[1,128]{1,0:T(1,128)S(1)}) custom-call(bf16[128,4608]{1,0:T(8,128)(2,1)S(1)} %copy-done.1, f32[1,128]{1,0:T(1,128)S(1)} %bitcast.7, bf16[64,4736]{1,0:T(8,128)(2,1)S(1)} %collective-permute-done.12.mine_ref, bf16[64,4736]{1,0:T(8,128)(2,1)S(1)} %collective-permute-done.13.other_ref), custom_call_target="tpu_custom_call" | custom-call | tf_op jit(solution)/shard_map/order/pallas_call | solution.py:264
  41.6 2.7 %conv.3 = (bf16[1280,128]{1,0:T(8,128)(2,1)S(1)}, bf16[320,512]{1,0:T(8,128)(2,1)S(1)}) custom-call(bf16[1440,128]{1,0:T(8,128)(2,1)S(1)} %collective-permute-done.8.first_ref, bf16[1440,128]{1,0:T(8,128)(2,1)S(1)} %collective-permute-done.9.crossed_ref, bf16[1440,128]{1,0:T(8,128)(2,1)S(1)} %collective-permute-done.10.second_ref, ...), custom_call_target="tpu_custom_call" | custom-call | tf_op jit(solution)/shard_map/conv/pallas_call | solution.py:292
  44.3 2.1 %conv.4 = (bf16[640,128]{1,0:T(8,128)(2,1)}, bf16[320,512]{1,0:T(8,128)(2,1)S(1)}) custom-call(bf16[640,128]{1,0:T(8,128)(2,1)S(1)} %collective-permute-done.4.first_ref, bf16[640,128]{1,0:T(8,128)(2,1)S(1)} %collective-permute-done.5.crossed_ref, bf16[640,128]{1,0:T(8,128)(2,1)S(1)} %collective-permute-done.6.second_ref, ...), custom_call_target="tpu_custom_call" | custom-call | tf_op jit(solution)/shard_map/conv/pallas_call | solution.py:292
  46.4 0.8 %collective-permute-start.17 = (bf16[640,128]{1,0:T(8,128)(2,1)}, bf16[640,128]{1,0:T(8,128)(2,1)S(1)}, u32[]{:S(2)}, u32[]{:S(2)}) collective-permute-start(bf16[640,128]{1,0:T(8,128)(2,1)} %get-tuple-element.25), channel_id=1, source_target_pairs={{0,1},{1,5},{2,3},{3,7},{4,0},{5,4},{6,2},{7,6},{8,9},{9,13},{10,1... | collective-permute-start | bytes 491528 | tf_op jit(solution)/shard_map/ppermute | solution.py:307
  47.2 1.7 %collective-permute-start.18 = (bf16[640,128]{1,0:T(8,128)(2,1)}, bf16[640,128]{1,0:T(8,128)(2,1)S(1)}, u32[]{:S(2)}, u32[]{:S(2)}) collective-permute-start(bf16[640,128]{1,0:T(8,128)(2,1)} %get-tuple-element.25), channel_id=1, source_target_pairs={{0,9},{1,13},{2,11},{3,15},{4,8},{5,12},{6,10},{7,14},{8,17},{9,21... | collective-permute-start | bytes 491528 | tf_op jit(solution)/shard_map/ppermute | solution.py:308
  48.9 0.8 %collective-permute-start.20 = (bf16[1280,128]{1,0:T(8,128)(2,1)S(1)}, bf16[1280,128]{1,0:T(8,128)(2,1)S(1)}, u32[]{:S(2)}, u32[]{:S(2)}) collective-permute-start(bf16[1280,128]{1,0:T(8,128)(2,1)S(1)} %get-tuple-element.26), channel_id=1, source_target_pairs={{0,1},{1,5},{2,3},{3,7},{4,0},{5,4},{6,2},{7,6},{8,9},{9,13},{10,1... | collective-permute-start | bytes 983048 | tf_op jit(solution)/shard_map/ppermute | solution.py:307
  49.6 0.9 %collective-permute-start.21 = (bf16[1280,128]{1,0:T(8,128)(2,1)S(1)}, bf16[1280,128]{1,0:T(8,128)(2,1)S(1)}, u32[]{:S(2)}, u32[]{:S(2)}) collective-permute-start(bf16[1280,128]{1,0:T(8,128)(2,1)S(1)} %get-tuple-element.26), channel_id=1, source_target_pairs={{0,9},{1,13},{2,11},{3,15},{4,8},{5,12},{6,10},{7,14},{8,17},{9,21... | collective-permute-start | bytes 983048 | tf_op jit(solution)/shard_map/ppermute | solution.py:308
  50.6 1.4 %conv.5 = (bf16[640,128]{1,0:T(8,128)(2,1)S(1)}, bf16[320,512]{1,0:T(8,128)(2,1)}) custom-call(bf16[480,128]{1,0:T(8,128)(2,1)S(1)} %collective-permute-done.first_ref, bf16[480,128]{1,0:T(8,128)(2,1)S(1)} %collective-permute-done.1.crossed_ref, bf16[480,128]{1,0:T(8,128)(2,1)S(1)} %collective-permute-done.2.second_ref, ...), custom_call_target="tpu_custom_call" | custom-call | tf_op jit(solution)/shard_map/conv/pallas_call | solution.py:292
  52.0 1.7 %collective-permute-start.14 = (bf16[640,128]{1,0:T(8,128)(2,1)S(1)}, bf16[640,128]{1,0:T(8,128)(2,1)S(1)}, u32[]{:S(2)}, u32[]{:S(2)}) collective-permute-start(bf16[640,128]{1,0:T(8,128)(2,1)S(1)} %get-tuple-element.24), channel_id=1, source_target_pairs={{0,1},{1,5},{2,3},{3,7},{4,0},{5,4},{6,2},{7,6},{8,9},{9,13},{10,1... | collective-permute-start | bytes 491528 | tf_op jit(solution)/shard_map/ppermute | solution.py:307
  53.7 1.0 %collective-permute-start.15 = (bf16[640,128]{1,0:T(8,128)(2,1)S(1)}, bf16[640,128]{1,0:T(8,128)(2,1)S(1)}, u32[]{:S(2)}, u32[]{:S(2)}) collective-permute-start(bf16[640,128]{1,0:T(8,128)(2,1)S(1)} %get-tuple-element.24), channel_id=1, source_target_pairs={{0,9},{1,13},{2,11},{3,15},{4,8},{5,12},{6,10},{7,14},{8,17},{9,21... | collective-permute-start | bytes 491528 | tf_op jit(solution)/shard_map/ppermute | solution.py:308
  54.8 0.6 collective-permute-start.19
  55.6 6.3 %collective-permute-done.21.before_ref = bf16[1280,128]{1,0:T(8,128)(2,1)S(1)} collective-permute-done((bf16[1280,128]{1,0:T(8,128)(2,1)S(1)}, bf16[1280,128]{1,0:T(8,128)(2,1)S(1)}, u32[]{:S(2)}, u32[]{:S(2)}) %collective-permute-start.21) | collective-permute-done | bytes 327712 | tf_op jit(solution)/shard_map/ppermute | solution.py:308
  62.0 3.4 %collective-permute-done.15.before_ref = bf16[640,128]{1,0:T(8,128)(2,1)S(1)} collective-permute-done((bf16[640,128]{1,0:T(8,128)(2,1)S(1)}, bf16[640,128]{1,0:T(8,128)(2,1)S(1)}, u32[]{:S(2)}, u32[]{:S(2)}) %collective-permute-start.15) | collective-permute-done | bytes 163872 | tf_op jit(solution)/shard_map/ppermute | solution.py:308
  65.5 1.0 %taps.3.refs_0_ = bf16[128,2560]{1,0:T(8,128)(2,1)} custom-call(bf16[1280,128]{1,0:T(8,128)(2,1)S(1)} %collective-permute-done.20.values_ref, bf16[1280,128]{1,0:T(8,128)(2,1)S(1)} %collective-permute-done.21.before_ref, bf16[1280,128]{1,0:T(8,128)(2,1)S(1)} %collective-permute-done.22.previous_ref, f32[3,128]{1,0:T(4,128)S(1)} %copy-done.3, ...), custom_call_target="tpu_custom_call" | custom-call | tf_op jit(solution)/shard_map/taps/pallas_call | solution.py:312
  66.5 0.9 %taps.4.refs_0_ = bf16[128,2560]{1,0:T(8,128)(2,1)} custom-call(bf16[640,128]{1,0:T(8,128)(2,1)S(1)} %collective-permute-done.17.values_ref, bf16[640,128]{1,0:T(8,128)(2,1)S(1)} %collective-permute-done.18.before_ref, bf16[640,128]{1,0:T(8,128)(2,1)S(1)} %collective-permute-done.19.previous_ref, ...), custom_call_target="tpu_custom_call", output_to_operand_aliasing={{}: (5, {})} | custom-call | tf_op jit(solution)/shard_map/taps/pallas_call | solution.py:312
  67.4 0.9 %taps.5 = bf16[128,2560]{1,0:T(8,128)(2,1)} custom-call(bf16[640,128]{1,0:T(8,128)(2,1)S(1)} %collective-permute-done.14.values_ref, bf16[640,128]{1,0:T(8,128)(2,1)S(1)} %collective-permute-done.15.before_ref, bf16[640,128]{1,0:T(8,128)(2,1)S(1)} %collective-permute-done.16.previous_ref, f32[3,128]{1,0:T(4,128)S(1)} %copy-done.3, ...), custom_call_target="tpu_custom_call", output_to_operand_aliasing={{}: (5, {})} | custom-call | tf_op jit(solution)/shard_map/taps/pallas_call | solution.py:312
  (38 shorter events, 1.0 us)
Async XLA Ops:
  0.0 1.3 %copy-start = (bf16[128,4608]{1,0:T(8,128)(2,1)S(1)}, bf16[128,4608]{1,0:T(8,128)(2,1)}, u32[]{:S(2)}) copy-start(bf16[128,4608]{1,0:T(8,128)(2,1)} %w_ref.3) | copy-start | bytes 3538948
  1.3 1.1 %copy-start.2 = (bf16[1,128,2560]{2,1,0:T(8,128)(2,1)S(1)}, bf16[1,128,2560]{2,1,0:T(8,128)(2,1)}, u32[]{:S(2)}) copy-start(bf16[1,128,2560]{2,1,0:T(8,128)(2,1)} %latent_ref.1) | copy-start | bytes 1966084
  2.4 0.7 copy-start.5
  3.0 37.8 %copy-start.1 = (bf16[128,4608]{1,0:T(8,128)(2,1)S(1)}, bf16[128,4608]{1,0:T(8,128)(2,1)}, u32[]{:S(2)}) copy-start(bf16[128,4608]{1,0:T(8,128)(2,1)} %w_ref.3) | copy-start | bytes 3538948
  3.8 12.4 %collective-permute-start.12 = (bf16[64,4736]{1,0:T(8,128)(2,1)S(1)}, bf16[64,4736]{1,0:T(8,128)(2,1)S(1)}, u32[]{:S(2)}, u32[]{:S(2)}) collective-permute-start(bf16[64,4736]{1,0:T(8,128)(2,1)S(1)} %get-tuple-element.19), channel_id=1, source_target_pairs={{1,0},{5,1},{3,2},{7,3},{0,4},{4,5},{2,6},{6,7},{9,8},{13,9},{11,1... | collective-permute-start | bytes 1818632 | tf_op jit(solution)/shard_map/ppermute | solution.py:262
  4.4 21.0 %collective-permute-start.10 = (bf16[1440,128]{1,0:T(8,128)(2,1)S(1)}, bf16[1440,128]{1,0:T(8,128)(2,1)S(1)}, u32[]{:S(2)}, u32[]{:S(2)}) collective-permute-start(bf16[1440,128]{1,0:T(8,128)(2,1)S(1)} %get-tuple-element.18.own_ref), channel_id=1, source_target_pairs={{0,4},{1,2},{2,6},{3,0},{4,7},{5,1},{6,5},{7,3},{8,12},{9,10},{10,... | collective-permute-start | bytes 1105928 | tf_op jit(solution)/shard_map/ppermute | solution.py:283
  6.5 20.0 %collective-permute-start.8 = (bf16[1440,128]{1,0:T(8,128)(2,1)S(1)}, bf16[1440,128]{1,0:T(8,128)(2,1)S(1)}, u32[]{:S(2)}, u32[]{:S(2)}) collective-permute-start(bf16[1440,128]{1,0:T(8,128)(2,1)S(1)} %get-tuple-element.18.own_ref), channel_id=1, source_target_pairs={{0,2},{1,4},{2,0},{3,6},{4,1},{5,7},{6,3},{7,5},{8,10},{9,12},{10,... | collective-permute-start | bytes 1105928 | tf_op jit(solution)/shard_map/ppermute | solution.py:282
  16.2 23.7 %collective-permute-start.13 = (bf16[64,4736]{1,0:T(8,128)(2,1)S(1)}, bf16[64,4736]{1,0:T(8,128)(2,1)S(1)}, u32[]{:S(2)}, u32[]{:S(2)}) collective-permute-start(bf16[64,4736]{1,0:T(8,128)(2,1)S(1)} %collective-permute-done.12.mine_ref), channel_id=1, source_target_pairs={{0,8},{1,1},{2,10},{3,3},{4,4},{5,13},{6,6},{7,15},{8,0},{9,9},{10... | collective-permute-start | bytes 1818632 | tf_op jit(solution)/shard_map/ppermute | solution.py:263
  25.4 14.5 %collective-permute-start.11 = (bf16[1440,128]{1,0:T(8,128)(2,1)S(1)}, bf16[1440,128]{1,0:T(8,128)(2,1)S(1)}, u32[]{:S(2)}, u32[]{:S(2)}) collective-permute-start(bf16[1440,128]{1,0:T(8,128)(2,1)S(1)} %collective-permute-done.10.second_ref), channel_id=1, source_target_pairs={{0,4},{4,0},{8,12},{12,8},{16,20},{20,16},{24,28},{28,24},{1,5},{5... | collective-permute-start | bytes 1105928 | tf_op jit(solution)/shard_map/ppermute | solution.py:239
  25.4 6.3 %collective-permute-start = (bf16[480,128]{1,0:T(8,128)(2,1)S(1)}, bf16[480,128]{1,0:T(8,128)(2,1)S(1)}, u32[]{:S(2)}, u32[]{:S(2)}) collective-permute-start(bf16[480,128]{1,0:T(8,128)(2,1)S(1)} %get-tuple-element.16.own_ref), channel_id=1, source_target_pairs={{0,2},{1,4},{2,0},{3,6},{4,1},{5,7},{6,3},{7,5},{8,10},{9,12},{10,... | collective-permute-start | bytes 368648 | tf_op jit(solution)/shard_map/ppermute | solution.py:282
  26.5 15.1 %collective-permute-start.9 = (bf16[1440,128]{1,0:T(8,128)(2,1)S(1)}, bf16[1440,128]{1,0:T(8,128)(2,1)S(1)}, u32[]{:S(2)}, u32[]{:S(2)}) collective-permute-start(bf16[1440,128]{1,0:T(8,128)(2,1)S(1)} %collective-permute-done.8.first_ref), channel_id=1, source_target_pairs={{0,4},{4,0},{8,12},{12,8},{16,20},{20,16},{24,28},{28,24},{1,5},{5... | collective-permute-start | bytes 1105928 | tf_op jit(solution)/shard_map/ppermute | solution.py:239
  26.9 12.4 %collective-permute-start.4 = (bf16[640,128]{1,0:T(8,128)(2,1)S(1)}, bf16[640,128]{1,0:T(8,128)(2,1)S(1)}, u32[]{:S(2)}, u32[]{:S(2)}) collective-permute-start(bf16[640,128]{1,0:T(8,128)(2,1)S(1)} %get-tuple-element.17.own_ref), channel_id=1, source_target_pairs={{0,2},{1,4},{2,0},{3,6},{4,1},{5,7},{6,3},{7,5},{8,10},{9,12},{10,... | collective-permute-start | bytes 491528 | tf_op jit(solution)/shard_map/ppermute | solution.py:282
  31.7 7.7 %collective-permute-start.6 = (bf16[640,128]{1,0:T(8,128)(2,1)S(1)}, bf16[640,128]{1,0:T(8,128)(2,1)S(1)}, u32[]{:S(2)}, u32[]{:S(2)}) collective-permute-start(bf16[640,128]{1,0:T(8,128)(2,1)S(1)} %get-tuple-element.17.own_ref), channel_id=1, source_target_pairs={{0,4},{1,2},{2,6},{3,0},{4,7},{5,1},{6,5},{7,3},{8,12},{9,10},{10,... | collective-permute-start | bytes 491528 | tf_op jit(solution)/shard_map/ppermute | solution.py:283
  39.3 5.0 %collective-permute-start.5 = (bf16[640,128]{1,0:T(8,128)(2,1)S(1)}, bf16[640,128]{1,0:T(8,128)(2,1)S(1)}, u32[]{:S(2)}, u32[]{:S(2)}) collective-permute-start(bf16[640,128]{1,0:T(8,128)(2,1)S(1)} %collective-permute-done.4.first_ref), channel_id=1, source_target_pairs={{0,4},{4,0},{8,12},{12,8},{16,20},{20,16},{24,28},{28,24},{1,5},{5... | collective-permute-start | bytes 491528 | tf_op jit(solution)/shard_map/ppermute | solution.py:239
  39.3 5.0 %collective-permute-start.7 = (bf16[640,128]{1,0:T(8,128)(2,1)S(1)}, bf16[640,128]{1,0:T(8,128)(2,1)S(1)}, u32[]{:S(2)}, u32[]{:S(2)}) collective-permute-start(bf16[640,128]{1,0:T(8,128)(2,1)S(1)} %collective-permute-done.6.second_ref), channel_id=1, source_target_pairs={{0,4},{4,0},{8,12},{12,8},{16,20},{20,16},{24,28},{28,24},{1,5},{5... | collective-permute-start | bytes 491528 | tf_op jit(solution)/shard_map/ppermute | solution.py:239
  39.9 9.0 %collective-permute-start.2 = (bf16[480,128]{1,0:T(8,128)(2,1)S(1)}, bf16[480,128]{1,0:T(8,128)(2,1)S(1)}, u32[]{:S(2)}, u32[]{:S(2)}) collective-permute-start(bf16[480,128]{1,0:T(8,128)(2,1)S(1)} %get-tuple-element.16.own_ref), channel_id=1, source_target_pairs={{0,4},{1,2},{2,6},{3,0},{4,7},{5,1},{6,5},{7,3},{8,12},{9,10},{10,... | collective-permute-start | bytes 368648 | tf_op jit(solution)/shard_map/ppermute | solution.py:283
  39.9 9.7 %collective-permute-start.1 = (bf16[480,128]{1,0:T(8,128)(2,1)S(1)}, bf16[480,128]{1,0:T(8,128)(2,1)S(1)}, u32[]{:S(2)}, u32[]{:S(2)}) collective-permute-start(bf16[480,128]{1,0:T(8,128)(2,1)S(1)} %collective-permute-done.first_ref), channel_id=1, source_target_pairs={{0,4},{4,0},{8,12},{12,8},{16,20},{20,16},{24,28},{28,24},{1,5},{5... | collective-permute-start | bytes 368648 | tf_op jit(solution)/shard_map/ppermute | solution.py:239
  46.4 7.3 %collective-permute-start.17 = (bf16[640,128]{1,0:T(8,128)(2,1)}, bf16[640,128]{1,0:T(8,128)(2,1)S(1)}, u32[]{:S(2)}, u32[]{:S(2)}) collective-permute-start(bf16[640,128]{1,0:T(8,128)(2,1)} %get-tuple-element.25), channel_id=1, source_target_pairs={{0,1},{1,5},{2,3},{3,7},{4,0},{5,4},{6,2},{7,6},{8,9},{9,13},{10,1... | collective-permute-start | bytes 491528 | tf_op jit(solution)/shard_map/ppermute | solution.py:307
  47.2 7.6 %collective-permute-start.18 = (bf16[640,128]{1,0:T(8,128)(2,1)}, bf16[640,128]{1,0:T(8,128)(2,1)S(1)}, u32[]{:S(2)}, u32[]{:S(2)}) collective-permute-start(bf16[640,128]{1,0:T(8,128)(2,1)} %get-tuple-element.25), channel_id=1, source_target_pairs={{0,9},{1,13},{2,11},{3,15},{4,8},{5,12},{6,10},{7,14},{8,17},{9,21... | collective-permute-start | bytes 491528 | tf_op jit(solution)/shard_map/ppermute | solution.py:308
  48.9 1.7 %collective-permute-start.3 = (bf16[480,128]{1,0:T(8,128)(2,1)S(1)}, bf16[480,128]{1,0:T(8,128)(2,1)S(1)}, u32[]{:S(2)}, u32[]{:S(2)}) collective-permute-start(bf16[480,128]{1,0:T(8,128)(2,1)S(1)} %collective-permute-done.2.second_ref), channel_id=1, source_target_pairs={{0,4},{4,0},{8,12},{12,8},{16,20},{20,16},{24,28},{28,24},{1,5},{5... | collective-permute-start | bytes 368648 | tf_op jit(solution)/shard_map/ppermute | solution.py:239
  48.9 6.7 %collective-permute-start.20 = (bf16[1280,128]{1,0:T(8,128)(2,1)S(1)}, bf16[1280,128]{1,0:T(8,128)(2,1)S(1)}, u32[]{:S(2)}, u32[]{:S(2)}) collective-permute-start(bf16[1280,128]{1,0:T(8,128)(2,1)S(1)} %get-tuple-element.26), channel_id=1, source_target_pairs={{0,1},{1,5},{2,3},{3,7},{4,0},{5,4},{6,2},{7,6},{8,9},{9,13},{10,1... | collective-permute-start | bytes 983048 | tf_op jit(solution)/shard_map/ppermute | solution.py:307
  49.6 12.2 %collective-permute-start.21 = (bf16[1280,128]{1,0:T(8,128)(2,1)S(1)}, bf16[1280,128]{1,0:T(8,128)(2,1)S(1)}, u32[]{:S(2)}, u32[]{:S(2)}) collective-permute-start(bf16[1280,128]{1,0:T(8,128)(2,1)S(1)} %get-tuple-element.26), channel_id=1, source_target_pairs={{0,9},{1,13},{2,11},{3,15},{4,8},{5,12},{6,10},{7,14},{8,17},{9,21... | collective-permute-start | bytes 983048 | tf_op jit(solution)/shard_map/ppermute | solution.py:308
  52.0 13.5 %copy-start.3 = (f32[3,128]{1,0:T(4,128)S(1)}, f32[3,128]{1,0:T(4,128)}, u32[]{:S(2)}) copy-start(f32[3,128]{1,0:T(4,128)} %taps_ref.5) | copy-start | bytes 4612
  52.0 13.5 %copy-start.4 = (f32[128]{0:T(128)S(1)}, f32[128]{0:T(128)}, u32[]{:S(2)}) copy-start(f32[128]{0:T(128)} %param.9) | copy-start | bytes 1540
  52.0 10.0 %collective-permute-start.14 = (bf16[640,128]{1,0:T(8,128)(2,1)S(1)}, bf16[640,128]{1,0:T(8,128)(2,1)S(1)}, u32[]{:S(2)}, u32[]{:S(2)}) collective-permute-start(bf16[640,128]{1,0:T(8,128)(2,1)S(1)} %get-tuple-element.24), channel_id=1, source_target_pairs={{0,1},{1,5},{2,3},{3,7},{4,0},{5,4},{6,2},{7,6},{8,9},{9,13},{10,1... | collective-permute-start | bytes 491528 | tf_op jit(solution)/shard_map/ppermute | solution.py:307
  53.7 11.6 %collective-permute-start.15 = (bf16[640,128]{1,0:T(8,128)(2,1)S(1)}, bf16[640,128]{1,0:T(8,128)(2,1)S(1)}, u32[]{:S(2)}, u32[]{:S(2)}) collective-permute-start(bf16[640,128]{1,0:T(8,128)(2,1)S(1)} %get-tuple-element.24), channel_id=1, source_target_pairs={{0,9},{1,13},{2,11},{3,15},{4,8},{5,12},{6,10},{7,14},{8,17},{9,21... | collective-permute-start | bytes 491528 | tf_op jit(solution)/shard_map/ppermute | solution.py:308
  54.8 11.7 %collective-permute-start.19 = (bf16[640,128]{1,0:T(8,128)(2,1)S(1)}, bf16[640,128]{1,0:T(8,128)(2,1)S(1)}, u32[]{:S(2)}, u32[]{:S(2)}) collective-permute-start(bf16[640,128]{1,0:T(8,128)(2,1)S(1)} %broadcast_select_fusion.1), channel_id=1, source_target_pairs={{0,4},{4,0},{8,12},{12,8},{16,20},{20,16},{24,28},{28,24},{1,5},{5... | collective-permute-start | bytes 491528 | tf_op jit(solution)/shard_map/ppermute | solution.py:239
  61.9 3.6 %collective-permute-start.22 = (bf16[1280,128]{1,0:T(8,128)(2,1)S(1)}, bf16[1280,128]{1,0:T(8,128)(2,1)S(1)}, u32[]{:S(2)}, u32[]{:S(2)}) collective-permute-start(bf16[1280,128]{1,0:T(8,128)(2,1)S(1)} %broadcast_select_fusion), channel_id=1, source_target_pairs={{0,4},{4,0},{8,12},{12,8},{16,20},{20,16},{24,28},{28,24},{1,5},{5... | collective-permute-start | bytes 983048 | tf_op jit(solution)/shard_map/ppermute | solution.py:239
  65.4 2.0 %collective-permute-start.16 = (bf16[640,128]{1,0:T(8,128)(2,1)S(1)}, bf16[640,128]{1,0:T(8,128)(2,1)S(1)}, u32[]{:S(2)}, u32[]{:S(2)}) collective-permute-start(bf16[640,128]{1,0:T(8,128)(2,1)S(1)} %broadcast_select_fusion.2), channel_id=1, source_target_pairs={{0,4},{4,0},{8,12},{12,8},{16,20},{20,16},{24,28},{28,24},{1,5},{5... | collective-permute-start | bytes 491528 | tf_op jit(solution)/shard_map/ppermute | solution.py:239

commit v2 on v1

--- a/solution.py
+++ b/solution.py
@@ -14,6 +14,7 @@
 
 VMEM = pl.BlockSpec(memory_space=pltpu.VMEM)
 ANY = pl.BlockSpec(memory_space=pl.ANY)
+HBM = pl.BlockSpec(memory_space=pltpu.HBM)
 
 
 def three_taps(history, values, temporal_w, temporal_b):
@@ -70,7 +71,7 @@
 
 
 def split_kernel(latent_ref, w_ref, b_ref, half_ref, *refs, starts, stops):
-    own_refs, (frame_ref, sems) = refs[:-2], refs[-2:]
+    own_refs, (frame_ref, bias_ref, sems) = refs[:-3], refs[-3:]
     side = place()[4]
     half, width = half_ref.shape[0], w_ref.shape[1]
     outs = w_ref.shape[0]
@@ -79,10 +80,15 @@
         [
             (w_ref.at[pl.ds(first, half), :], half_ref.at[:, 0:width]),
             (latent_ref.at[0], frame_ref),
+            (b_ref, bias_ref),
         ],
         sems,
     )
-    bias = b_ref[...]
+    moves[1].wait()
+    for own_ref, a, b in zip(own_refs, starts, stops):
+        own_ref[...] = frame_ref[:, a * W : b * W].T
+    moves[2].wait()
+    bias = bias_ref[...]
     high = bias.astype(jnp.bfloat16)
     rest = bias - high.astype(jnp.float32)
     middle = rest.astype(jnp.bfloat16)
@@ -98,9 +104,6 @@
         ),
     ).T
     half_ref[:, width:] = jnp.where(side == 0, pieces[0:half], pieces[half:]).astype(jnp.bfloat16)
-    moves[1].wait()
-    for own_ref, a, b in zip(own_refs, starts, stops):
-        own_ref[...] = frame_ref[:, a * W : b * W].T
     moves[0].wait()
 
 
@@ -119,9 +122,8 @@
 
     @pl.when(jnp.logical_not(straight))
     def _():
-        for move in copies([(w_ref, rows_ref.at[:, 0:width])], sems):
+        for move in copies([(w_ref, rows_ref.at[:, 0:width]), (b_ref, bias_ref)], sems):
             move.wait()
-        bias_ref[...] = b_ref[...]
 
     @pl.when(straight)
     def _():
@@ -190,8 +192,8 @@
     out_ref[...] = (left + total[:, outs : 2 * outs] + right + b_ref[...]).astype(out_ref.dtype)
 
 
-def taps_kernel(values_ref, before_ref, previous_ref, taps_ref, bias_ref, *refs):
-    out_ref = refs[-1]
+def taps_kernel(values_ref, before_ref, previous_ref, taps_ref, bias_ref, *refs, column):
+    decoded_ref, out_ref, sem = refs[-3:]
     frame = place()[1]
     before = jnp.where(frame >= 2, before_ref[...].astype(jnp.float32), 0.0)
     previous = jnp.where(frame >= 1, previous_ref[...].astype(jnp.float32), 0.0)
@@ -202,6 +204,14 @@
         + taps_ref[2:3, :] * values_ref[...].astype(jnp.float32)
     )
     out_ref[...] = total.astype(out_ref.dtype).T
+    target = decoded_ref.at[:, column : column + out_ref.shape[1]]
+    move = pltpu.make_async_copy(out_ref, target, sem)
+    move.start()
+    move.wait()
+
+
+def in_hbm(x):
+    return pltpu.with_memory_space_constraint(x, pltpu.HBM)
 
 
 def limit(mib):
@@ -230,10 +240,13 @@
     out = [(b, a) for a, b in home]
     ahead = [(a, (b + 8) % (4 * frame_count)) for a, b in home]
     pair = [(f, f ^ 1) for f in range(frame_count)]
+    behind = []
+    for (a, b), (_, c) in zip(home, ahead):
+        behind.append((a, b + 4 if b // 4 % 2 == 0 else c - 4))
     across = []
     for f in range(frame_count):
         for z in range(4):
-            across.append((f * 4 + z, (f ^ 2 if z % 2 == f % 2 else f) * 4 + z))
+            across.append((f * 4 + z, (f ^ 2 if z % 2 == f % 2 else f ^ 4) * 4 + z))
 
     def swap(x):
         return lax.ppermute(x, "frame", pair)
@@ -249,15 +262,16 @@
             jax.ShapeDtypeStruct(((b - a) * W, local_chan), jnp.bfloat16)
             for a, b in zip(starts, stops)
         ],
-        in_specs=[ANY, ANY, VMEM],
+        in_specs=[HBM, HBM, HBM],
         out_specs=[VMEM] * (1 + len(starts)),
         scratch_shapes=[
             pltpu.VMEM((local_chan, pixels), jnp.bfloat16),
-            pltpu.SemaphoreType.DMA((2,)),
+            pltpu.VMEM((1, outs), jnp.float32),
+            pltpu.SemaphoreType.DMA((3,)),
         ],
         compiler_params=limit(8),
         name="split",
-    )(latent, spatial_w, bias_row)
+    )(in_hbm(latent), in_hbm(spatial_w), in_hbm(bias_row))
 
     mine = lax.ppermute(mine, both, out)
     other = lax.ppermute(mine, both, across)
@@ -267,7 +281,7 @@
             jax.ShapeDtypeStruct((3, 4 * local_chan, 3 * outs), jnp.bfloat16),
             jax.ShapeDtypeStruct((1, outs), jnp.float32),
         ),
-        in_specs=[ANY, VMEM, ANY, ANY],
+        in_specs=[HBM, HBM, ANY, ANY],
         out_specs=(VMEM, VMEM),
         scratch_shapes=[
             pltpu.VMEM((outs, width + 128), jnp.bfloat16),
@@ -275,7 +289,7 @@
         ],
         compiler_params=limit(8),
         name="order",
-    )(spatial_w, bias_row, mine, other)
+    )(in_hbm(spatial_w), in_hbm(bias_row), mine, other)
 
     arrived = []
     for own in owns:
@@ -306,15 +320,20 @@
         )(first, crossed, second, own, passed, tail, filters, bias)
         spatial = lax.ppermute(done, both, home)
         before = lax.ppermute(done, both, ahead)
-        previous = swap(jnp.where(core == 1, before, spatial))
+        if low:
+            previous = lax.ppermute(done, both, behind)
+        else:
+            previous = swap(jnp.where(core == 1, before, spatial))
         held = [] if decoded is None else [decoded]
-        block = column // size
         decoded = pl.pallas_call(
-            taps_kernel,
+            functools.partial(taps_kernel, column=column),
             out_shape=jax.ShapeDtypeStruct((outs, pixels), jnp.bfloat16),
-            grid=(1,),
-            in_specs=[VMEM] * 5 + [ANY] * len(held),
-            out_specs=pl.BlockSpec((outs, size), lambda n, block=block: (0, block)),
+            in_specs=[VMEM] * 5 + [HBM] * len(held),
+            out_specs=HBM,
+            scratch_shapes=[
+                pltpu.VMEM((outs, size), jnp.bfloat16),
+                pltpu.SemaphoreType.DMA,
+            ],
             input_output_aliases={5: 0} if held else {},
             compiler_params=limit(8),
             name="taps",
@@ -324,7 +343,7 @@
 
 
 def shards(latent, *rest):
-    if lax.axis_size("chan") == 4 and lax.axis_size("frame") % 4 == 0 and latent.shape[0] == 1:
+    if lax.axis_size("chan") == 4 and lax.axis_size("frame") % 8 == 0 and latent.shape[0] == 1:
         return split_work(latent, *rest)
     return gathered(latent, *rest)
 

time: 68.5 us -> 67.2 us (0.981)
  starting transfers between devices: 24.1 us -> 27.7 us
  local copies, waits for them, and re-layouts: 3.05 us -> 0.04 us
  waiting for transfers between devices: 30.5 us -> 27.5 us
  Pallas kernels: 10.4 us -> 11.5 us
    ppermute x3, waiting for transfers between devices: 5.13 us -> 12.5 us  [split_work(): second = lax.ppermute(own, both, far)]
    ppermute x3, waiting for transfers between devices: 8.25 us -> 1.19 us  [split_work(): first = lax.ppermute(own, both, near)]
    ppermute x9 -> x8, starting transfers between devices: 2.59 us -> 7.94 us  [swap(): return lax.ppermute(x, 'frame', pair)]
    ppermute x3, waiting for transfers between devices: 9.73 us -> 6.62 us  [split_work(): before = lax.ppermute(done, both, ahead)]
    unnamed x12 -> x4, local copies, waits for them, and re-layouts: 3.03 us -> 0.01 us
    ppermute x3, starting transfers between devices: 3.27 us -> 5.83 us  [split_work(): spatial = lax.ppermute(done, both, home)]
    ppermute x3, starting transfers between devices: 3.62 us -> 1.23 us  [split_work(): before = lax.ppermute(done, both, ahead)]
    ppermute x0 -> x1, starting transfers between devices: none -> 2.08 us  [split_work(): previous = lax.ppermute(done, both, behind)]
  transfers between devices with their start and end apart: 23 -> 23, of which waited for: 8 -> 7; matrix products, arithmetic and copies ran while one was open for 0% -> 0% of each run, Pallas kernels for 13% -> 13%
where the time goes in v2:
time: 67.2 us; the launch traced here: 67.1 us
  starting transfers between devices  27.7 us (41%)
  waiting for transfers between devices  27.5 us (41%)
  Pallas kernels  11.5 us (17%)
    ppermute x3, waiting for transfers between devices, split_work(): second = lax.ppermute(own, both, far)  12.5 us
    ppermute x8, starting transfers between devices, swap(): return lax.ppermute(x, 'frame', pair)  7.94 us
    ppermute x1, waiting for transfers between devices, split_work(): mine = lax.ppermute(mine, both, out)  7.17 us
    ppermute x3, waiting for transfers between devices, split_work(): before = lax.ppermute(done, both, ahead)  6.62 us
    pallas_call x3, Pallas kernels, split_work(): pl.pallas_call(functools.partial(conv_kernel, top=k == 0, low=low), out_s...  6.21 us
    ppermute x3, starting transfers between devices, split_work(): first = lax.ppermute(own, both, near)  5.86 us
    ppermute x3, starting transfers between devices, split_work(): spatial = lax.ppermute(done, both, home)  5.83 us
    pallas_call x3, Pallas kernels, split_work(): pl.pallas_call(functools.partial(taps_kernel, column=column), out_shape=j...  2.77 us
  transfers between devices with their start and end apart: 23, of which 7 were waited for; matrix products, arithmetic and copies ran while one was open for 0% of the time, Pallas kernels for 13%

profile of v2, /device:TPU:0, one launch (start us, length us, event | category | flops | bytes accessed | tf_op | source)
XLA Modules:
  0.0 67.1 jit_solution(13737069209002066020)
XLA Ops:
  0.0 1.8 %split.1 = (bf16[64,4736]{1,0:T(8,128)(2,1)S(1)}, bf16[1440,128]{1,0:T(8,128)(2,1)S(1)}, bf16[640,128]{1,0:T(8,128)(2,1)S(1)}, bf16[480,128]{1,0:T(8,128)(2,1)S(1)}) custom-call(bf16[1,128,2560]{2,1,0:T(8,128)(2,1)} %latent_ref.1, bf16[128,4608]{1,0:T(8,128)(2,1)} %w_ref.3, f32[1,128]{1,0:T(1,128)} %bitcast.6), custom_call_target="tpu_custom_call" | custom-call | tf_op jit(solution)/shard_map/split/pallas_call | solution.py:258
  1.8 0.6 collective-permute-start.12
  2.4 2.1 %collective-permute-start.10 = (bf16[1440,128]{1,0:T(8,128)(2,1)S(1)}, bf16[1440,128]{1,0:T(8,128)(2,1)S(1)}, u32[]{:S(2)}, u32[]{:S(2)}) collective-permute-start(bf16[1440,128]{1,0:T(8,128)(2,1)S(1)} %get-tuple-element.18.own_ref), channel_id=1, source_target_pairs={{0,4},{1,2},{2,6},{3,0},{4,7},{5,1},{6,5},{7,3},{8,12},{9,10},{10,... | collective-permute-start | bytes 1105928 | tf_op jit(solution)/shard_map/ppermute | solution.py:297
  4.5 2.6 %collective-permute-start.8 = (bf16[1440,128]{1,0:T(8,128)(2,1)S(1)}, bf16[1440,128]{1,0:T(8,128)(2,1)S(1)}, u32[]{:S(2)}, u32[]{:S(2)}) collective-permute-start(bf16[1440,128]{1,0:T(8,128)(2,1)S(1)} %get-tuple-element.18.own_ref), channel_id=1, source_target_pairs={{0,2},{1,4},{2,0},{3,6},{4,1},{5,7},{6,3},{7,5},{8,10},{9,12},{10,... | collective-permute-start | bytes 1105928 | tf_op jit(solution)/shard_map/ppermute | solution.py:296
  7.1 7.2 %collective-permute-done.12.mine_ref = bf16[64,4736]{1,0:T(8,128)(2,1)S(1)} collective-permute-done((bf16[64,4736]{1,0:T(8,128)(2,1)S(1)}, bf16[64,4736]{1,0:T(8,128)(2,1)S(1)}, u32[]{:S(2)}, u32[]{:S(2)}) %collective-permute-start.12) | collective-permute-done | bytes 606240 | tf_op jit(solution)/shard_map/ppermute | solution.py:276
  14.3 2.1 %collective-permute-start.13 = (bf16[64,4736]{1,0:T(8,128)(2,1)S(1)}, bf16[64,4736]{1,0:T(8,128)(2,1)S(1)}, u32[]{:S(2)}, u32[]{:S(2)}) collective-permute-start(bf16[64,4736]{1,0:T(8,128)(2,1)S(1)} %collective-permute-done.12.mine_ref), channel_id=1, source_target_pairs={{0,8},{1,17},{2,10},{3,19},{4,20},{5,13},{6,22},{7,15},{8,0},{9,25... | collective-permute-start | bytes 1818632 | tf_op jit(solution)/shard_map/ppermute | solution.py:277
  16.3 7.0 %collective-permute-done.10.second_ref = bf16[1440,128]{1,0:T(8,128)(2,1)S(1)} collective-permute-done((bf16[1440,128]{1,0:T(8,128)(2,1)S(1)}, bf16[1440,128]{1,0:T(8,128)(2,1)S(1)}, u32[]{:S(2)}, u32[]{:S(2)}) %collective-permute-start.10) | collective-permute-done | bytes 368672 | tf_op jit(solution)/shard_map/ppermute | solution.py:297
  23.4 0.5 collective-permute-done.8.first_ref
  23.8 0.8 %collective-permute-start.9 = (bf16[1440,128]{1,0:T(8,128)(2,1)S(1)}, bf16[1440,128]{1,0:T(8,128)(2,1)S(1)}, u32[]{:S(2)}, u32[]{:S(2)}) collective-permute-start(bf16[1440,128]{1,0:T(8,128)(2,1)S(1)} %collective-permute-done.8.first_ref), channel_id=1, source_target_pairs={{0,4},{4,0},{8,12},{12,8},{16,20},{20,16},{24,28},{28,24},{1,5},{5... | collective-permute-start | bytes 1105928 | tf_op jit(solution)/shard_map/ppermute | solution.py:252
  24.7 3.2 %collective-permute-start.4 = (bf16[640,128]{1,0:T(8,128)(2,1)S(1)}, bf16[640,128]{1,0:T(8,128)(2,1)S(1)}, u32[]{:S(2)}, u32[]{:S(2)}) collective-permute-start(bf16[640,128]{1,0:T(8,128)(2,1)S(1)} %get-tuple-element.17.own_ref), channel_id=1, source_target_pairs={{0,2},{1,4},{2,0},{3,6},{4,1},{5,7},{6,3},{7,5},{8,10},{9,12},{10,... | collective-permute-start | bytes 491528 | tf_op jit(solution)/shard_map/ppermute | solution.py:296
  27.9 0.7 %order.1 = (bf16[3,512,384]{2,1,0:T(8,128)(2,1)S(1)}, f32[1,128]{1,0:T(1,128)S(1)}) custom-call(bf16[128,4608]{1,0:T(8,128)(2,1)} %w_ref.3, f32[1,128]{1,0:T(1,128)} %bitcast.7, bf16[64,4736]{1,0:T(8,128)(2,1)S(1)} %collective-permute-done.12.mine_ref, bf16[64,4736]{1,0:T(8,128)(2,1)S(1)} %collective-permute-done.13.other_ref), custom_call_target="tpu_custom_call" | custom-call | tf_op jit(solution)/shard_map/order/pallas_call | solution.py:278
  28.7 3.4 %conv.3 = (bf16[1280,128]{1,0:T(8,128)(2,1)}, bf16[320,512]{1,0:T(8,128)(2,1)S(1)}) custom-call(bf16[1440,128]{1,0:T(8,128)(2,1)S(1)} %collective-permute-done.8.first_ref, bf16[1440,128]{1,0:T(8,128)(2,1)S(1)} %collective-permute-done.9.crossed_ref, bf16[1440,128]{1,0:T(8,128)(2,1)S(1)} %collective-permute-done.10.second_ref, ...), custom_call_target="tpu_custom_call" | custom-call | tf_op jit(solution)/shard_map/conv/pallas_call | solution.py:306
  32.2 4.4 %collective-permute-start.20 = (bf16[1280,128]{1,0:T(8,128)(2,1)}, bf16[1280,128]{1,0:T(8,128)(2,1)S(1)}, u32[]{:S(2)}, u32[]{:S(2)}) collective-permute-start(bf16[1280,128]{1,0:T(8,128)(2,1)} %get-tuple-element.26), channel_id=1, source_target_pairs={{0,1},{1,5},{2,3},{3,7},{4,0},{5,4},{6,2},{7,6},{8,9},{9,13},{10,1... | collective-permute-start | bytes 983048 | tf_op jit(solution)/shard_map/ppermute | solution.py:321
  36.6 1.1 %collective-permute-start.21 = (bf16[1280,128]{1,0:T(8,128)(2,1)}, bf16[1280,128]{1,0:T(8,128)(2,1)S(1)}, u32[]{:S(2)}, u32[]{:S(2)}) collective-permute-start(bf16[1280,128]{1,0:T(8,128)(2,1)} %get-tuple-element.26), channel_id=1, source_target_pairs={{0,9},{1,13},{2,11},{3,15},{4,8},{5,12},{6,10},{7,14},{8,17},{9,21... | collective-permute-start | bytes 983048 | tf_op jit(solution)/shard_map/ppermute | solution.py:322
  37.6 0.6 collective-permute-start.5
  38.2 0.7 %collective-permute-done.first_ref = bf16[480,128]{1,0:T(8,128)(2,1)S(1)} collective-permute-done((bf16[480,128]{1,0:T(8,128)(2,1)S(1)}, bf16[480,128]{1,0:T(8,128)(2,1)S(1)}, u32[]{:S(2)}, u32[]{:S(2)}) %collective-permute-start) | collective-permute-done | bytes 122912 | tf_op jit(solution)/shard_map/ppermute | solution.py:296
  39.0 1.4 %collective-permute-start.7 = (bf16[640,128]{1,0:T(8,128)(2,1)S(1)}, bf16[640,128]{1,0:T(8,128)(2,1)S(1)}, u32[]{:S(2)}, u32[]{:S(2)}) collective-permute-start(bf16[640,128]{1,0:T(8,128)(2,1)S(1)} %collective-permute-done.6.second_ref), channel_id=1, source_target_pairs={{0,4},{4,0},{8,12},{12,8},{16,20},{20,16},{24,28},{28,24},{1,5},{5... | collective-permute-start | bytes 491528 | tf_op jit(solution)/shard_map/ppermute | solution.py:252
  40.3 5.5 %collective-permute-done.2.second_ref = bf16[480,128]{1,0:T(8,128)(2,1)S(1)} collective-permute-done((bf16[480,128]{1,0:T(8,128)(2,1)S(1)}, bf16[480,128]{1,0:T(8,128)(2,1)S(1)}, u32[]{:S(2)}, u32[]{:S(2)}) %collective-permute-start.2) | collective-permute-done | bytes 122912 | tf_op jit(solution)/shard_map/ppermute | solution.py:297
  45.8 0.5 collective-permute-start.3
  46.3 1.4 %conv.4 = (bf16[640,128]{1,0:T(8,128)(2,1)S(1)}, bf16[320,512]{1,0:T(8,128)(2,1)S(1)}) custom-call(bf16[640,128]{1,0:T(8,128)(2,1)S(1)} %collective-permute-done.4.first_ref, bf16[640,128]{1,0:T(8,128)(2,1)S(1)} %collective-permute-done.5.crossed_ref, bf16[640,128]{1,0:T(8,128)(2,1)S(1)} %collective-permute-done.6.second_ref, ...), custom_call_target="tpu_custom_call" | custom-call | tf_op jit(solution)/shard_map/conv/pallas_call | solution.py:306
  47.8 0.1 collective-permute-start.18
  47.9 1.4 %conv.5 = (bf16[640,128]{1,0:T(8,128)(2,1)S(1)}, bf16[320,512]{1,0:T(8,128)(2,1)}) custom-call(bf16[480,128]{1,0:T(8,128)(2,1)S(1)} %collective-permute-done.first_ref, bf16[480,128]{1,0:T(8,128)(2,1)S(1)} %collective-permute-done.1.crossed_ref, bf16[480,128]{1,0:T(8,128)(2,1)S(1)} %collective-permute-done.2.second_ref, ...), custom_call_target="tpu_custom_call" | custom-call | tf_op jit(solution)/shard_map/conv/pallas_call | solution.py:306
  49.4 2.5 %collective-permute-start.22 = (bf16[1280,128]{1,0:T(8,128)(2,1)S(1)}, bf16[1280,128]{1,0:T(8,128)(2,1)S(1)}, u32[]{:S(2)}, u32[]{:S(2)}) collective-permute-start(bf16[1280,128]{1,0:T(8,128)(2,1)S(1)} %broadcast_select_fusion), channel_id=1, source_target_pairs={{0,4},{4,0},{8,12},{12,8},{16,20},{20,16},{24,28},{28,24},{1,5},{5... | collective-permute-start | bytes 983048 | tf_op jit(solution)/shard_map/ppermute | solution.py:252
  51.9 1.6 %collective-permute-done.18.before_ref = bf16[640,128]{1,0:T(8,128)(2,1)S(1)} collective-permute-done((bf16[640,128]{1,0:T(8,128)(2,1)S(1)}, bf16[640,128]{1,0:T(8,128)(2,1)S(1)}, u32[]{:S(2)}, u32[]{:S(2)}) %collective-permute-start.18) | collective-permute-done | bytes 163872 | tf_op jit(solution)/shard_map/ppermute | solution.py:322
  53.5 2.2 %collective-permute-start.19 = (bf16[640,128]{1,0:T(8,128)(2,1)S(1)}, bf16[640,128]{1,0:T(8,128)(2,1)S(1)}, u32[]{:S(2)}, u32[]{:S(2)}) collective-permute-start(bf16[640,128]{1,0:T(8,128)(2,1)S(1)} %broadcast_select_fusion.1), channel_id=1, source_target_pairs={{0,4},{4,0},{8,12},{12,8},{16,20},{20,16},{24,28},{28,24},{1,5},{5... | collective-permute-start | bytes 491528 | tf_op jit(solution)/shard_map/ppermute | solution.py:252
  55.7 1.3 %collective-permute-start.14 = (bf16[640,128]{1,0:T(8,128)(2,1)S(1)}, bf16[640,128]{1,0:T(8,128)(2,1)S(1)}, u32[]{:S(2)}, u32[]{:S(2)}) collective-permute-start(bf16[640,128]{1,0:T(8,128)(2,1)S(1)} %get-tuple-element.24), channel_id=1, source_target_pairs={{0,1},{1,5},{2,3},{3,7},{4,0},{5,4},{6,2},{7,6},{8,9},{9,13},{10,1... | collective-permute-start | bytes 491528 | tf_op jit(solution)/shard_map/ppermute | solution.py:321
  57.0 0.1 collective-permute-start.15
  57.2 2.1 %collective-permute-start.16 = (bf16[640,128]{1,0:T(8,128)(2,1)S(1)}, bf16[640,128]{1,0:T(8,128)(2,1)S(1)}, u32[]{:S(2)}, u32[]{:S(2)}) collective-permute-start(bf16[640,128]{1,0:T(8,128)(2,1)S(1)} %get-tuple-element.24), channel_id=1, source_target_pairs={{0,5},{1,9},{2,7},{3,11},{4,4},{5,8},{6,6},{7,10},{8,13},{9,17},{1... | collective-permute-start | bytes 491528 | tf_op jit(solution)/shard_map/ppermute | solution.py:324
  59.3 1.0 %taps.3.refs_0_ = bf16[128,2560]{1,0:T(8,128)(2,1)} custom-call(bf16[1280,128]{1,0:T(8,128)(2,1)S(1)} %collective-permute-done.20.values_ref, bf16[1280,128]{1,0:T(8,128)(2,1)S(1)} %collective-permute-done.21.before_ref, bf16[1280,128]{1,0:T(8,128)(2,1)S(1)} %collective-permute-done.22.previous_ref, f32[3,128]{1,0:T(4,128)S(1)} %copy-done, f32[1,128]{1,0:T(1,128)S(1)} %bitcast.3), custom_call_target="tpu_custom_call" | custom-call | tf_op jit(solution)/shard_map/taps/pallas_call | solution.py:328
  60.3 0.9 %taps.4.refs_0_ = bf16[128,2560]{1,0:T(8,128)(2,1)} custom-call(bf16[640,128]{1,0:T(8,128)(2,1)S(1)} %collective-permute-done.17.values_ref, bf16[640,128]{1,0:T(8,128)(2,1)S(1)} %collective-permute-done.18.before_ref, bf16[640,128]{1,0:T(8,128)(2,1)S(1)} %collective-permute-done.19.previous_ref, ...), custom_call_target="tpu_custom_call", output_to_operand_aliasing={{}: (5, {})} | custom-call | tf_op jit(solution)/shard_map/taps/pallas_call | solution.py:328
  61.2 5.0 %collective-permute-done.15.before_ref = bf16[640,128]{1,0:T(8,128)(2,1)S(1)} collective-permute-done((bf16[640,128]{1,0:T(8,128)(2,1)S(1)}, bf16[640,128]{1,0:T(8,128)(2,1)S(1)}, u32[]{:S(2)}, u32[]{:S(2)}) %collective-permute-start.15) | collective-permute-done | bytes 163872 | tf_op jit(solution)/shard_map/ppermute | solution.py:322
  66.2 0.9 %taps.5 = bf16[128,2560]{1,0:T(8,128)(2,1)} custom-call(bf16[640,128]{1,0:T(8,128)(2,1)S(1)} %collective-permute-done.14.values_ref, bf16[640,128]{1,0:T(8,128)(2,1)S(1)} %collective-permute-done.15.before_ref, bf16[640,128]{1,0:T(8,128)(2,1)S(1)} %collective-permute-done.16.previous_ref, f32[3,128]{1,0:T(4,128)S(1)} %copy-done, ...), custom_call_target="tpu_custom_call", output_to_operand_aliasing={{}: (5, {})} | custom-call | tf_op jit(solution)/shard_map/taps/pallas_call | solution.py:328
  (29 shorter events, 0.2 us)
Async XLA Ops:
  1.8 12.4 %collective-permute-start.12 = (bf16[64,4736]{1,0:T(8,128)(2,1)S(1)}, bf16[64,4736]{1,0:T(8,128)(2,1)S(1)}, u32[]{:S(2)}, u32[]{:S(2)}) collective-permute-start(bf16[64,4736]{1,0:T(8,128)(2,1)S(1)} %get-tuple-element.19), channel_id=1, source_target_pairs={{1,0},{5,1},{3,2},{7,3},{0,4},{4,5},{2,6},{6,7},{9,8},{13,9},{11,1... | collective-permute-start | bytes 1818632 | tf_op jit(solution)/shard_map/ppermute | solution.py:276
  2.4 21.0 %collective-permute-start.10 = (bf16[1440,128]{1,0:T(8,128)(2,1)S(1)}, bf16[1440,128]{1,0:T(8,128)(2,1)S(1)}, u32[]{:S(2)}, u32[]{:S(2)}) collective-permute-start(bf16[1440,128]{1,0:T(8,128)(2,1)S(1)} %get-tuple-element.18.own_ref), channel_id=1, source_target_pairs={{0,4},{1,2},{2,6},{3,0},{4,7},{5,1},{6,5},{7,3},{8,12},{9,10},{10,... | collective-permute-start | bytes 1105928 | tf_op jit(solution)/shard_map/ppermute | solution.py:297
  4.5 19.3 %collective-permute-start.8 = (bf16[1440,128]{1,0:T(8,128)(2,1)S(1)}, bf16[1440,128]{1,0:T(8,128)(2,1)S(1)}, u32[]{:S(2)}, u32[]{:S(2)}) collective-permute-start(bf16[1440,128]{1,0:T(8,128)(2,1)S(1)} %get-tuple-element.18.own_ref), channel_id=1, source_target_pairs={{0,2},{1,4},{2,0},{3,6},{4,1},{5,7},{6,3},{7,5},{8,10},{9,12},{10,... | collective-permute-start | bytes 1105928 | tf_op jit(solution)/shard_map/ppermute | solution.py:296
  14.3 13.7 %collective-permute-start.13 = (bf16[64,4736]{1,0:T(8,128)(2,1)S(1)}, bf16[64,4736]{1,0:T(8,128)(2,1)S(1)}, u32[]{:S(2)}, u32[]{:S(2)}) collective-permute-start(bf16[64,4736]{1,0:T(8,128)(2,1)S(1)} %collective-permute-done.12.mine_ref), channel_id=1, source_target_pairs={{0,8},{1,17},{2,10},{3,19},{4,20},{5,13},{6,22},{7,15},{8,0},{9,25... | collective-permute-start | bytes 1818632 | tf_op jit(solution)/shard_map/ppermute | solution.py:277
  23.4 5.3 %collective-permute-start.11 = (bf16[1440,128]{1,0:T(8,128)(2,1)S(1)}, bf16[1440,128]{1,0:T(8,128)(2,1)S(1)}, u32[]{:S(2)}, u32[]{:S(2)}) collective-permute-start(bf16[1440,128]{1,0:T(8,128)(2,1)S(1)} %collective-permute-done.10.second_ref), channel_id=1, source_target_pairs={{0,4},{4,0},{8,12},{12,8},{16,20},{20,16},{24,28},{28,24},{1,5},{5... | collective-permute-start | bytes 1105928 | tf_op jit(solution)/shard_map/ppermute | solution.py:252
  23.8 4.9 %collective-permute-start.9 = (bf16[1440,128]{1,0:T(8,128)(2,1)S(1)}, bf16[1440,128]{1,0:T(8,128)(2,1)S(1)}, u32[]{:S(2)}, u32[]{:S(2)}) collective-permute-start(bf16[1440,128]{1,0:T(8,128)(2,1)S(1)} %collective-permute-done.8.first_ref), channel_id=1, source_target_pairs={{0,4},{4,0},{8,12},{12,8},{16,20},{20,16},{24,28},{28,24},{1,5},{5... | collective-permute-start | bytes 1105928 | tf_op jit(solution)/shard_map/ppermute | solution.py:252
  24.7 13.0 %collective-permute-start.4 = (bf16[640,128]{1,0:T(8,128)(2,1)S(1)}, bf16[640,128]{1,0:T(8,128)(2,1)S(1)}, u32[]{:S(2)}, u32[]{:S(2)}) collective-permute-start(bf16[640,128]{1,0:T(8,128)(2,1)S(1)} %get-tuple-element.17.own_ref), channel_id=1, source_target_pairs={{0,2},{1,4},{2,0},{3,6},{4,1},{5,7},{6,3},{7,5},{8,10},{9,12},{10,... | collective-permute-start | bytes 491528 | tf_op jit(solution)/shard_map/ppermute | solution.py:296
  27.9 11.1 %collective-permute-start = (bf16[480,128]{1,0:T(8,128)(2,1)S(1)}, bf16[480,128]{1,0:T(8,128)(2,1)S(1)}, u32[]{:S(2)}, u32[]{:S(2)}) collective-permute-start(bf16[480,128]{1,0:T(8,128)(2,1)S(1)} %get-tuple-element.16.own_ref), channel_id=1, source_target_pairs={{0,2},{1,4},{2,0},{3,6},{4,1},{5,7},{6,3},{7,5},{8,10},{9,12},{10,... | collective-permute-start | bytes 368648 | tf_op jit(solution)/shard_map/ppermute | solution.py:296
  27.9 11.0 %collective-permute-start.6 = (bf16[640,128]{1,0:T(8,128)(2,1)S(1)}, bf16[640,128]{1,0:T(8,128)(2,1)S(1)}, u32[]{:S(2)}, u32[]{:S(2)}) collective-permute-start(bf16[640,128]{1,0:T(8,128)(2,1)S(1)} %get-tuple-element.17.own_ref), channel_id=1, source_target_pairs={{0,4},{1,2},{2,6},{3,0},{4,7},{5,1},{6,5},{7,3},{8,12},{9,10},{10,... | collective-permute-start | bytes 491528 | tf_op jit(solution)/shard_map/ppermute | solution.py:297
  32.2 17.2 %collective-permute-start.20 = (bf16[1280,128]{1,0:T(8,128)(2,1)}, bf16[1280,128]{1,0:T(8,128)(2,1)S(1)}, u32[]{:S(2)}, u32[]{:S(2)}) collective-permute-start(bf16[1280,128]{1,0:T(8,128)(2,1)} %get-tuple-element.26), channel_id=1, source_target_pairs={{0,1},{1,5},{2,3},{3,7},{4,0},{5,4},{6,2},{7,6},{8,9},{9,13},{10,1... | collective-permute-start | bytes 983048 | tf_op jit(solution)/shard_map/ppermute | solution.py:321
  36.6 12.8 %collective-permute-start.21 = (bf16[1280,128]{1,0:T(8,128)(2,1)}, bf16[1280,128]{1,0:T(8,128)(2,1)S(1)}, u32[]{:S(2)}, u32[]{:S(2)}) collective-permute-start(bf16[1280,128]{1,0:T(8,128)(2,1)} %get-tuple-element.26), channel_id=1, source_target_pairs={{0,9},{1,13},{2,11},{3,15},{4,8},{5,12},{6,10},{7,14},{8,17},{9,21... | collective-permute-start | bytes 983048 | tf_op jit(solution)/shard_map/ppermute | solution.py:322
  37.6 8.2 %collective-permute-start.5 = (bf16[640,128]{1,0:T(8,128)(2,1)S(1)}, bf16[640,128]{1,0:T(8,128)(2,1)S(1)}, u32[]{:S(2)}, u32[]{:S(2)}) collective-permute-start(bf16[640,128]{1,0:T(8,128)(2,1)S(1)} %collective-permute-done.4.first_ref), channel_id=1, source_target_pairs={{0,4},{4,0},{8,12},{12,8},{16,20},{20,16},{24,28},{28,24},{1,5},{5... | collective-permute-start | bytes 491528 | tf_op jit(solution)/shard_map/ppermute | solution.py:252
  39.0 6.8 %collective-permute-start.2 = (bf16[480,128]{1,0:T(8,128)(2,1)S(1)}, bf16[480,128]{1,0:T(8,128)(2,1)S(1)}, u32[]{:S(2)}, u32[]{:S(2)}) collective-permute-start(bf16[480,128]{1,0:T(8,128)(2,1)S(1)} %get-tuple-element.16.own_ref), channel_id=1, source_target_pairs={{0,4},{1,2},{2,6},{3,0},{4,7},{5,1},{6,5},{7,3},{8,12},{9,10},{10,... | collective-permute-start | bytes 368648 | tf_op jit(solution)/shard_map/ppermute | solution.py:297
  39.0 7.3 %collective-permute-start.7 = (bf16[640,128]{1,0:T(8,128)(2,1)S(1)}, bf16[640,128]{1,0:T(8,128)(2,1)S(1)}, u32[]{:S(2)}, u32[]{:S(2)}) collective-permute-start(bf16[640,128]{1,0:T(8,128)(2,1)S(1)} %collective-permute-done.6.second_ref), channel_id=1, source_target_pairs={{0,4},{4,0},{8,12},{12,8},{16,20},{20,16},{24,28},{28,24},{1,5},{5... | collective-permute-start | bytes 491528 | tf_op jit(solution)/shard_map/ppermute | solution.py:252
  45.8 2.0 %collective-permute-start.1 = (bf16[480,128]{1,0:T(8,128)(2,1)S(1)}, bf16[480,128]{1,0:T(8,128)(2,1)S(1)}, u32[]{:S(2)}, u32[]{:S(2)}) collective-permute-start(bf16[480,128]{1,0:T(8,128)(2,1)S(1)} %collective-permute-done.first_ref), channel_id=1, source_target_pairs={{0,4},{4,0},{8,12},{12,8},{16,20},{20,16},{24,28},{28,24},{1,5},{5... | collective-permute-start | bytes 368648 | tf_op jit(solution)/shard_map/ppermute | solution.py:252
  45.8 2.1 %collective-permute-start.3 = (bf16[480,128]{1,0:T(8,128)(2,1)S(1)}, bf16[480,128]{1,0:T(8,128)(2,1)}, u32[]{:S(2)}, u32[]{:S(2)}) collective-permute-start(bf16[480,128]{1,0:T(8,128)(2,1)S(1)} %collective-permute-done.2.second_ref), channel_id=1, source_target_pairs={{0,4},{4,0},{8,12},{12,8},{16,20},{20,16},{24,28},{28,24},{1,5},{5... | collective-permute-start | bytes 368648 | tf_op jit(solution)/shard_map/ppermute | solution.py:252
  47.7 4.2 %collective-permute-start.17 = (bf16[640,128]{1,0:T(8,128)(2,1)S(1)}, bf16[640,128]{1,0:T(8,128)(2,1)S(1)}, u32[]{:S(2)}, u32[]{:S(2)}) collective-permute-start(bf16[640,128]{1,0:T(8,128)(2,1)S(1)} %get-tuple-element.25), channel_id=1, source_target_pairs={{0,1},{1,5},{2,3},{3,7},{4,0},{5,4},{6,2},{7,6},{8,9},{9,13},{10,1... | collective-permute-start | bytes 491528 | tf_op jit(solution)/shard_map/ppermute | solution.py:321
  47.8 5.7 %collective-permute-start.18 = (bf16[640,128]{1,0:T(8,128)(2,1)S(1)}, bf16[640,128]{1,0:T(8,128)(2,1)S(1)}, u32[]{:S(2)}, u32[]{:S(2)}) collective-permute-start(bf16[640,128]{1,0:T(8,128)(2,1)S(1)} %get-tuple-element.25), channel_id=1, source_target_pairs={{0,9},{1,13},{2,11},{3,15},{4,8},{5,12},{6,10},{7,14},{8,17},{9,21... | collective-permute-start | bytes 491528 | tf_op jit(solution)/shard_map/ppermute | solution.py:322
  49.3 10.0 %copy-start = (f32[3,128]{1,0:T(4,128)S(1)}, f32[3,128]{1,0:T(4,128)}, u32[]{:S(2)}) copy-start(f32[3,128]{1,0:T(4,128)} %taps_ref.5) | copy-start | bytes 4612
  49.3 10.0 %copy-start.1 = (f32[128]{0:T(128)S(1)}, f32[128]{0:T(128)}, u32[]{:S(2)}) copy-start(f32[128]{0:T(128)} %param.9) | copy-start | bytes 1540
  49.4 9.9 %collective-permute-start.22 = (bf16[1280,128]{1,0:T(8,128)(2,1)S(1)}, bf16[1280,128]{1,0:T(8,128)(2,1)S(1)}, u32[]{:S(2)}, u32[]{:S(2)}) collective-permute-start(bf16[1280,128]{1,0:T(8,128)(2,1)S(1)} %broadcast_select_fusion), channel_id=1, source_target_pairs={{0,4},{4,0},{8,12},{12,8},{16,20},{20,16},{24,28},{28,24},{1,5},{5... | collective-permute-start | bytes 983048 | tf_op jit(solution)/shard_map/ppermute | solution.py:252
  53.5 6.8 %collective-permute-start.19 = (bf16[640,128]{1,0:T(8,128)(2,1)S(1)}, bf16[640,128]{1,0:T(8,128)(2,1)S(1)}, u32[]{:S(2)}, u32[]{:S(2)}) collective-permute-start(bf16[640,128]{1,0:T(8,128)(2,1)S(1)} %broadcast_select_fusion.1), channel_id=1, source_target_pairs={{0,4},{4,0},{8,12},{12,8},{16,20},{20,16},{24,28},{28,24},{1,5},{5... | collective-permute-start | bytes 491528 | tf_op jit(solution)/shard_map/ppermute | solution.py:252
  55.7 5.5 %collective-permute-start.14 = (bf16[640,128]{1,0:T(8,128)(2,1)S(1)}, bf16[640,128]{1,0:T(8,128)(2,1)S(1)}, u32[]{:S(2)}, u32[]{:S(2)}) collective-permute-start(bf16[640,128]{1,0:T(8,128)(2,1)S(1)} %get-tuple-element.24), channel_id=1, source_target_pairs={{0,1},{1,5},{2,3},{3,7},{4,0},{5,4},{6,2},{7,6},{8,9},{9,13},{10,1... | collective-permute-start | bytes 491528 | tf_op jit(solution)/shard_map/ppermute | solution.py:321
  57.0 9.2 %collective-permute-start.15 = (bf16[640,128]{1,0:T(8,128)(2,1)S(1)}, bf16[640,128]{1,0:T(8,128)(2,1)S(1)}, u32[]{:S(2)}, u32[]{:S(2)}) collective-permute-start(bf16[640,128]{1,0:T(8,128)(2,1)S(1)} %get-tuple-element.24), channel_id=1, source_target_pairs={{0,9},{1,13},{2,11},{3,15},{4,8},{5,12},{6,10},{7,14},{8,17},{9,21... | collective-permute-start | bytes 491528 | tf_op jit(solution)/shard_map/ppermute | solution.py:322
  57.2 9.0 %collective-permute-start.16 = (bf16[640,128]{1,0:T(8,128)(2,1)S(1)}, bf16[640,128]{1,0:T(8,128)(2,1)S(1)}, u32[]{:S(2)}, u32[]{:S(2)}) collective-permute-start(bf16[640,128]{1,0:T(8,128)(2,1)S(1)} %get-tuple-element.24), channel_id=1, source_target_pairs={{0,5},{1,9},{2,7},{3,11},{4,4},{5,8},{6,6},{7,10},{8,13},{9,17},{1... | collective-permute-start | bytes 491528 | tf_op jit(solution)/shard_map/ppermute | solution.py:324
